TPU v7x, 256 devices: a whole 4x4x8 slice. The times are simulated.
256 devices in a mesh: clip: 16 (over y, z_hi, core), space: 16 (over z_lo, x).
Axes of the slice: x: 4, y: 4, z: 8 (z_hi: 2, z_lo: 4; z = z_hi * 4 + z_lo), core: 2. Of those that a mesh axis runs over, the one named last changes fastest.
Arguments:
- teacher_input: bfloat16 [16, 2, 128, 32, 512], P('clip', None, 'space'), may hold values from -6 to 6
- conv_first: bfloat16 [3, 3, 3, 512, 256], replicated, may hold values from -0.0546875 to 0.0546875
- conv_second: bfloat16 [3, 3, 3, 256, 256], replicated, may hold values from -0.078125 to 0.078125
- student_low: bfloat16 [16, 2, 128, 32, 256], P('clip', None, 'space'), may hold values from -6 to 6
- student_high: bfloat16 [16, 2, 256, 64, 128], P('clip', None, 'space'), may hold values from -6 to 6
- kernel_low: float32 [3, 3, 3, 256], replicated, may hold values from -1 to 1
- kernel_high: float32 [3, 3, 3, 128], replicated, may hold values from -1 to 1
- adapter_low: bfloat16 [256, 256], replicated, may hold values from -0.0078125 to 0.0078125
- adapter_high: bfloat16 [128, 256], replicated, may hold values from -0.009765625 to 0.009765625
Outputs:
- adapter_low_gradient: float32 [256, 256], P('clip')
- kernel_low_gradient: float32 [3, 3, 3, 256], P(None, None, None, 'clip')
- adapter_high_gradient: float32 [128, 256], P('clip')
- kernel_high_gradient: float32 [3, 3, 3, 128], P(None, None, None, 'clip')
- fine_mismatch: bfloat16 [16, 2, 256, 64, 256], P('clip', None, 'space')
All inputs are finite; a program needn't handle non-finite values.
Results may differ from a plain program's by a relative error of at most 0.0067.
Values may be sent and summed in bfloat16 or wider, within the bound.
A program may use at most 192 MiB of HBM per device.

v0:
```python
import jax
import jax.numpy as jnp
from jax import lax
from jax.sharding import PartitionSpec as P


def padded_2(block, sides, width):
    for axis, dim in sides:
        count = lax.axis_size(axis)
        forward = [(i, i + 1) for i in range(count - 1)]
        backward = [(target, source) for source, target in forward]
        low = lax.ppermute(
            lax.slice_in_dim(block, block.shape[dim] - width, None, axis=dim), axis, forward
        )
        high = lax.ppermute(lax.slice_in_dim(block, 0, width, axis=dim), axis, backward)
        block = jnp.concatenate([low, block, high], axis=dim)
    return block


def pad_sides(field):
    return jnp.pad(field, ((0, 0), (1, 1), (0, 0), (1, 1), (0, 0)))


def conv_taps(padded, weight, row_count):
    frames = padded.shape[1] - 2
    col_count = padded.shape[3] - 2
    summed = jnp.zeros(
        (padded.shape[0], frames, row_count, col_count, weight.shape[-1]), jnp.float32
    )
    for tap_t in range(3):
        for tap_h in range(3):
            for tap_w in range(3):
                window_part = padded[
                    :,
                    tap_t : tap_t + frames,
                    tap_h : tap_h + row_count,
                    tap_w : tap_w + col_count,
                    :,
                ]
                summed = summed + jnp.dot(
                    window_part, weight[tap_t, tap_h, tap_w], preferred_element_type=jnp.float32
                )
    return summed


def student_level(field, extended, kernel, adapter, target, scale):
    padded = pad_sides(extended)
    frames, row_count, col_count = (field.shape[1], field.shape[2], field.shape[3])
    mixed = field.astype(jnp.float32)
    for tap_t in range(3):
        for tap_h in range(3):
            for tap_w in range(3):
                shifted = padded[
                    :,
                    tap_t : tap_t + frames,
                    tap_h : tap_h + row_count,
                    tap_w : tap_w + col_count,
                    :,
                ]
                mixed = mixed + shifted.astype(jnp.float32) * kernel[tap_t, tap_h, tap_w]
    student = mixed.astype(jnp.bfloat16)
    output = jnp.dot(student, adapter, preferred_element_type=jnp.float32)
    mismatch = output - target.astype(jnp.float32)
    resid = (mismatch * scale).astype(jnp.bfloat16)
    adapter_part = jnp.einsum("bfhwc,bfhwd->cd", student, resid, preferred_element_type=jnp.float32)
    back = jnp.einsum("bfhwd,cd->bfhwc", resid, adapter, preferred_element_type=jnp.float32)
    kernel_rows = []
    for tap_t in range(3):
        for tap_h in range(3):
            for tap_w in range(3):
                shifted = padded[
                    :,
                    tap_t : tap_t + frames,
                    tap_h : tap_h + row_count,
                    tap_w : tap_w + col_count,
                    :,
                ]
                kernel_rows.append(jnp.sum(back * shifted.astype(jnp.float32), axis=(0, 1, 2, 3)))
    kernel_part = jnp.stack(kernel_rows).reshape(kernel.shape)
    return (adapter_part, kernel_part, mismatch.astype(jnp.bfloat16))


def on_device(
    teacher_input,
    conv_first,
    conv_second,
    student_low,
    student_high,
    kernel_low,
    kernel_high,
    adapter_low,
    adapter_high,
):
    row_count = teacher_input.shape[2]
    tiles = lax.axis_size("space")
    low_count = (
        teacher_input.shape[0]
        * teacher_input.shape[1]
        * row_count
        * teacher_input.shape[3]
        * lax.axis_size("clip")
        * tiles
    )
    scale_low = 1.0 / low_count
    scale_high = 1.0 / (4 * low_count)
    input_ext = padded_2(teacher_input, (("space", 2),), 1)
    first_feature = conv_taps(pad_sides(input_ext), conv_first, row_count).astype(jnp.bfloat16)
    feature_ext = padded_2(first_feature, (("space", 2),), 1)
    gated = jax.nn.silu(feature_ext.astype(jnp.float32)).astype(jnp.bfloat16)
    upsampled = jnp.repeat(jnp.repeat(gated, 2, axis=2), 2, axis=3)[:, :, 1 : 2 * row_count + 3]
    second_feature = conv_taps(pad_sides(upsampled), conv_second, 2 * row_count).astype(
        jnp.bfloat16
    )
    low_ext = padded_2(student_low, (("space", 2),), 1)
    high_ext = padded_2(student_high, (("space", 2),), 1)
    adapter_one, kernel_one, unused_low = student_level(
        student_low, low_ext, kernel_low, adapter_low, first_feature, scale_low
    )
    adapter_two, kernel_two, mismatch_two = student_level(
        student_high, high_ext, kernel_high, adapter_high, second_feature, scale_high
    )
    summed = lax.psum((adapter_one, adapter_two, kernel_one, kernel_two), "space")
    shares = (
        lax.psum_scatter(summed[0], "clip", scatter_dimension=0, tiled=True),
        lax.psum_scatter(summed[1], "clip", scatter_dimension=0, tiled=True),
        lax.psum_scatter(summed[2], "clip", scatter_dimension=3, tiled=True),
        lax.psum_scatter(summed[3], "clip", scatter_dimension=3, tiled=True),
    )
    return (shares[0], shares[2], shares[1], shares[3], mismatch_two)


def solution(mesh):
    in_specs = (
        P("clip", None, "space", None, None),
        P(),
        P(),
        P("clip", None, "space", None, None),
        P("clip", None, "space", None, None),
        P(),
        P(),
        P(),
        P(),
    )
    out_specs = (
        P("clip", None),
        P(None, None, None, "clip"),
        P("clip", None),
        P(None, None, None, "clip"),
        P("clip", None, "space", None, None),
    )
    return jax.shard_map(
        on_device, mesh=mesh, in_specs=in_specs, out_specs=out_specs, check_vma=False
    )
```

profile of v0, /device:TPU:2, one launch (start us, length us, event | category | flops | bytes accessed | tf_op | source)
XLA Modules:
  0.0 382.2 jit_solution(15966634600959560922)
XLA Ops:
  8.2 3.4 collective-permute-start.2
  11.6 2.4 collective-permute-start.3
  14.9 3.4 collective-permute-start.4
  18.3 2.4 collective-permute-start.5
  21.5 3.4 collective-permute-start
  29.7 2.4 collective-permute-start.1
  32.5 4.1 %collective-permute-done.1 = bf16[1,2,1,32,256]{4,3,2,1,0:T(8,128)(2,1)S(1)} collective-permute-done((bf16[1,2,1,32,256]{4,3,2,1,0:T(8,128)(2,1)S(1)}, bf16[1,2,1,32,256]{4,3,2,1,0:T(8,128)(2,1)S(1)}, u32[]{:S(2)}, u32[]{:S(2)}) %collective-permute-start.1) | collective-permute-done | bytes 32800 | tf_op jit(solution)/shard_map/ppermute | solution.py:15
  36.8 4.8 %fusion.93 = bf16[1,2,16,64,128]{4,3,2,1,0:T(8,128)(2,1)} fusion(bf16[1,2,16,64,128]{4,3,2,1,0:T(8,128)(2,1)S(1)} %copy-done.7, bf16[1,2,1,64,128]{4,3,2,1,0:T(8,128)(2,1)S(1)} %collective-permute-done.5, bf16[1,2,1,64,128]{4,3,2,1,0:T(8,128)(2,1)S(1)} %collective-permute-done.4, f32[128]{0:T(128)S(1)} %get-tuple-element.135, ...), kind=kLoop, calls=%fused_computation.198 | loop fusion | flops 22020096 | bytes 13710848 | tf_op jit(solution)/shard_map/convert_element_type | solution.py:61
  41.6 2.0 fusion.228
  52.9 6.0 %collective-permute-start.6 = (bf16[1,2,1,32,256]{4,3,1,2,0:T(8,128)(2,1)S(1)}, bf16[1,2,1,32,256]{4,3,1,2,0:T(8,128)(2,1)S(1)}, u32[]{:S(2)}, u32[]{:S(2)}) collective-permute-start(bf16[1,2,1,32,256]{4,3,1,2,0:T(8,128)(2,1)S(1)} %get-tuple-element.79), channel_id=1, source_target_pairs={{0,1},{1,2},{2,3},{3,4},{4,5},{5,6},{6,7},{7,8},{8,9},{9,10},{10,1... | collective-permute-start | bytes 98312 | tf_op jit(solution)/shard_map/ppermute | solution.py:12
  58.9 2.1 collective-permute-start.7
  64.7 2.5 reshape.625
  67.6 2.0 broadcast_in_dim.12
  69.6 4.1 %broadcast_in_dim.13 = bf16[1,2,20,64,256]{4,3,2,1,0:T(8,128)(2,1)} reshape(bf16[2,20,32,2,256]{4,3,2,1,0:T(2,128)(2,1)} %broadcast_in_dim.12) | data formatting | bytes 2621440 | tf_op jit(solution)/shard_map/broadcast_in_dim | solution.py:110
  75.2 2.7 fusion.100
  77.9 1.8 fusion.103
  83.2 1.8 fusion.112
  88.5 1.8 fusion.121
  92.1 1.9 fusion.127
  93.9 1.8 fusion.130
  99.2 1.8 fusion.139
  102.8 1.8 fusion.145
  106.4 1.8 fusion.151
  113.5 1.8 fusion.163
  120.5 1.8 fusion.169
  122.3 19.0 %add_convert_fusion = bf16[2,16,64,256]{3,2,1,0:T(8,128)(2,1)} fusion(f32[2,16,64,256]{3,2,1,0:T(8,128)} %fusion.163, f32[2,16,64,256]{3,2,1,0:T(8,128)} %fusion.160, f32[2,16,64,256]{3,2,1,0:T(8,128)} %fusion.157, f32[2,16,64,256]{3,2,1,0:T(8,128)} %fusion.154, f32[2,16,64,256]{3,2,1,0:T(8,128)} %fusion.151, f32[2,16,64,256]{3,2,1,0:T(8,128)} %fusion.148, ...), kind=kOutput, calls=%fused_computation.44 | convolution fusion | flops 282591232 | bytes 56885248 | tf_op jit(solution)/shard_map/dot_general | solution.py:40
  147.7 2.9 fusion.82
  150.7 2.7 fusion.94
  153.5 89.6 %all-reduce.4 = f32[3,3,3,128]{3,2,1,0:T(4,128)S(1)} all-reduce(f32[3,3,3,128]{3,2,1,0:T(4,128)S(1)} %reshape.566), channel_id=5, replica_groups=mesh['clip'=16,'space'=16] {'clip'}, use_global_device_ids=true, to_apply=%region_61.62.clone | all-reduce | flops 3456 | bytes 27648
  243.2 2.7 convert_bitcast_fusion
  246.9 56.0 %reduce-scatter.7.cloned.1.call-done = f32[16,256]{1,0:T(8,128)} async-done(((f32[256,256]{1,0:T(8,128)}), f32[16,256]{1,0:T(8,128)}) %reduce-scatter.7.cloned.1.call-update) | async-done | bytes 16400 | tf_op jit(solution)/shard_map/reduce_scatter | solution.py:124
  302.9 72.7 %all-reduce.5 = (f32[16,256]{1,0:T(8,128)}, f32[3,3,3,16]{3,2,1,0:T(4,128)}, f32[8,256]{1,0:T(8,128)}, f32[3,3,3,8]{3,2,1,0:T(4,128)}) all-reduce(f32[16,256]{1,0:T(8,128)} %reduce-scatter.7.cloned.1.call-done, f32[3,3,3,16]{3,2,1,0:T(4,128)S(1)} %copy.78, ...), channel_id=1, replica_groups=mesh['clip'=16,'space'=16] {'space'}, use_global_device_ids=true, to_apply=%region_0.1 | all-reduce | flops 6792 | bytes 54336 | tf_op jit(solution)/shard_map/psum | solution.py:122
  (123 shorter events, 55.4 us)
Async XLA Ops:
  7.2 53.9 %copy-start = (bf16[256,256]{1,0:T(8,128)(2,1)S(1)}, bf16[256,256]{1,0:T(8,128)(2,1)}, u32[]{:S(2)}) copy-start(bf16[256,256]{1,0:T(8,128)(2,1)} %param.16) | copy-start | bytes 393220
  7.2 25.0 %copy-start.7 = (bf16[1,2,16,64,128]{4,3,2,1,0:T(8,128)(2,1)S(1)}, bf16[1,2,16,64,128]{4,3,2,1,0:T(8,128)(2,1)}, u32[]{:S(2)}) copy-start(bf16[1,2,16,64,128]{4,3,2,1,0:T(8,128)(2,1)} %param.13) | copy-start | bytes 1572868
  7.2 29.4 %copy-start.9 = (bf16[1,2,8,32,256]{4,3,2,1,0:T(8,128)(2,1)S(1)}, bf16[1,2,8,32,256]{4,3,2,1,0:T(8,128)(2,1)}, u32[]{:S(2)}) copy-start(bf16[1,2,8,32,256]{4,3,2,1,0:T(8,128)(2,1)} %param.12) | copy-start | bytes 786436
  7.2 238.7 %reduce-scatter.11.cloned.1.call-start = ((), (), s32[]{:S(2)}) async-start(), calls=%async_computation.5 | async-start | bytes 139264
  8.2 35.4 %collective-permute-start.2 = (bf16[1,2,1,32,512]{4,3,2,1,0:T(8,128)(2,1)S(1)}, bf16[1,2,1,32,512]{4,3,2,1,0:T(8,128)(2,1)S(1)}, u32[]{:S(2)}, u32[]{:S(2)}) collective-permute-start(bf16[1,2,1,32,512]{4,3,2,1,0:T(8,128)(2,1)S(1)} %get-tuple-element.77), channel_id=1, source_target_pairs={{0,1},{1,2},{2,3},{3,4},{4,5},{5,6},{6,7},{7,8},{8,9},{9,10},{10,1... | collective-permute-start | bytes 196616 | tf_op jit(solution)/shard_map/ppermute | solution.py:12
  11.6 32.0 %collective-permute-start.3 = (bf16[1,2,1,32,512]{4,3,2,1,0:T(8,128)(2,1)S(1)}, bf16[1,2,1,32,512]{4,3,2,1,0:T(8,128)(2,1)S(1)}, u32[]{:S(2)}, u32[]{:S(2)}) collective-permute-start(bf16[1,2,1,32,512]{4,3,2,1,0:T(8,128)(2,1)S(1)} %get-tuple-element.78), channel_id=1, source_target_pairs={{1,0},{2,1},{3,2},{4,3},{5,4},{6,5},{7,6},{8,7},{9,8},{10,9},{11,1... | collective-permute-start | bytes 196616 | tf_op jit(solution)/shard_map/ppermute | solution.py:15
  14.9 14.8 %collective-permute-start.4 = (bf16[1,2,1,64,128]{4,3,2,1,0:T(8,128)(2,1)S(1)}, bf16[1,2,1,64,128]{4,3,2,1,0:T(8,128)(2,1)S(1)}, u32[]{:S(2)}, u32[]{:S(2)}) collective-permute-start(bf16[1,2,1,64,128]{4,3,2,1,0:T(8,128)(2,1)S(1)} %get-tuple-element.75), channel_id=1, source_target_pairs={{0,1},{1,2},{2,3},{3,4},{4,5},{5,6},{6,7},{7,8},{8,9},{9,10},{10,1... | collective-permute-start | bytes 98312 | tf_op jit(solution)/shard_map/ppermute | solution.py:12
  18.3 13.9 %collective-permute-start.5 = (bf16[1,2,1,64,128]{4,3,2,1,0:T(8,128)(2,1)S(1)}, bf16[1,2,1,64,128]{4,3,2,1,0:T(8,128)(2,1)S(1)}, u32[]{:S(2)}, u32[]{:S(2)}) collective-permute-start(bf16[1,2,1,64,128]{4,3,2,1,0:T(8,128)(2,1)S(1)} %get-tuple-element.76), channel_id=1, source_target_pairs={{1,0},{2,1},{3,2},{4,3},{5,4},{6,5},{7,6},{8,7},{9,8},{10,9},{11,1... | collective-permute-start | bytes 98312 | tf_op jit(solution)/shard_map/ppermute | solution.py:15
  21.5 11.0 %collective-permute-start = (bf16[1,2,1,32,256]{4,3,2,1,0:T(8,128)(2,1)S(1)}, bf16[1,2,1,32,256]{4,3,2,1,0:T(8,128)(2,1)S(1)}, u32[]{:S(2)}, u32[]{:S(2)}) collective-permute-start(bf16[1,2,1,32,256]{4,3,2,1,0:T(8,128)(2,1)S(1)} %get-tuple-element.81), channel_id=1, source_target_pairs={{0,1},{1,2},{2,3},{3,4},{4,5},{5,6},{6,7},{7,8},{8,9},{9,10},{10,1... | collective-permute-start | bytes 98312 | tf_op jit(solution)/shard_map/ppermute | solution.py:12
  29.7 6.9 %collective-permute-start.1 = (bf16[1,2,1,32,256]{4,3,2,1,0:T(8,128)(2,1)S(1)}, bf16[1,2,1,32,256]{4,3,2,1,0:T(8,128)(2,1)S(1)}, u32[]{:S(2)}, u32[]{:S(2)}) collective-permute-start(bf16[1,2,1,32,256]{4,3,2,1,0:T(8,128)(2,1)S(1)} %get-tuple-element.82), channel_id=1, source_target_pairs={{1,0},{2,1},{3,2},{4,3},{5,4},{6,5},{7,6},{8,7},{9,8},{10,9},{11,1... | collective-permute-start | bytes 98312 | tf_op jit(solution)/shard_map/ppermute | solution.py:15
  36.6 7.5 %slice-start = ((s8[7077888]{0:T(1024)(128)(4,1)}), s8[4194304]{0:T(1024)(128)(4,1)S(1)}, s32[]{:S(2)}) async-start(s8[7077888]{0:T(1024)(128)(4,1)} %bitcast.735), calls=%async_computation.6 | async-start | bytes 8388608
  36.8 7.3 %slice-start.1 = ((s8[7077888]{0:T(1024)(128)(4,1)}), s8[2883584]{0:T(1024)(128)(4,1)S(1)}, s32[]{:S(2)}) async-start(s8[7077888]{0:T(1024)(128)(4,1)} %bitcast.735), calls=%async_computation.7 | async-start | bytes 5767168
  41.6 2.1 copy-start.6
  43.6 17.4 %copy-start.10 = (bf16[1,2,8,32,256]{4,3,2,1,0:T(8,128)(2,1)}, bf16[1,2,8,32,256]{4,3,2,1,0:T(8,128)(2,1)S(1)}, u32[]{:S(2)}) copy-start(bf16[1,2,8,32,256]{4,3,2,1,0:T(8,128)(2,1)S(1)} %fusion.228) | copy-start | bytes 786436
  52.9 14.4 %collective-permute-start.6 = (bf16[1,2,1,32,256]{4,3,1,2,0:T(8,128)(2,1)S(1)}, bf16[1,2,1,32,256]{4,3,1,2,0:T(8,128)(2,1)S(1)}, u32[]{:S(2)}, u32[]{:S(2)}) collective-permute-start(bf16[1,2,1,32,256]{4,3,1,2,0:T(8,128)(2,1)S(1)} %get-tuple-element.79), channel_id=1, source_target_pairs={{0,1},{1,2},{2,3},{3,4},{4,5},{5,6},{6,7},{7,8},{8,9},{9,10},{10,1... | collective-permute-start | bytes 98312 | tf_op jit(solution)/shard_map/ppermute | solution.py:12
  58.9 8.4 %collective-permute-start.7 = (bf16[1,2,1,32,256]{4,3,1,2,0:T(8,128)(2,1)S(1)}, bf16[1,2,1,32,256]{4,3,1,2,0:T(8,128)(2,1)S(1)}, u32[]{:S(2)}, u32[]{:S(2)}) collective-permute-start(bf16[1,2,1,32,256]{4,3,1,2,0:T(8,128)(2,1)S(1)} %get-tuple-element.80), channel_id=1, source_target_pairs={{1,0},{2,1},{3,2},{4,3},{5,4},{6,5},{7,6},{8,7},{9,8},{10,9},{11,1... | collective-permute-start | bytes 98312 | tf_op jit(solution)/shard_map/ppermute | solution.py:15
  61.3 0.7 copy-start.12
  67.3 179.6 %reduce-scatter.9.cloned.1.call-start = ((), (), s32[]{:S(2)}) async-start(), calls=%async_computation.4 | async-start | bytes 139264 | tf_op jit(solution)/shard_map/reduce_scatter | solution.py:125
  73.7 4.2 %copy-start.5 = (bf16[3,3,3,256,256]{4,3,2,1,0:T(8,128)(2,1)S(1)}, bf16[3,3,3,256,256]{4,3,2,1,0:T(8,128)(2,1)}, u32[]{:S(2)}) copy-start(bf16[3,3,3,256,256]{4,3,2,1,0:T(8,128)(2,1)} %param.11) | copy-start | bytes 10616836
  115.3 1.7 copy-start.2
  122.3 19.1 %copy-start.4 = (bf16[1,2,16,64,128]{4,3,2,1,0:T(8,128)(2,1)S(1)}, bf16[1,2,16,64,128]{4,3,2,1,0:T(8,128)(2,1)}, u32[]{:S(2)}) copy-start(bf16[1,2,16,64,128]{4,3,2,1,0:T(8,128)(2,1)} %fusion.93) | copy-start | bytes 1572868
  122.3 19.1 %copy-start.14 = (bf16[128,256]{1,0:T(8,128)(2,1)S(1)}, bf16[128,256]{1,0:T(8,128)(2,1)}, u32[]{:S(2)}) copy-start(bf16[128,256]{1,0:T(8,128)(2,1)} %param.17) | copy-start | bytes 196612
  143.0 1.4 copy-start.3
  144.4 1.1 copy-start.15
  144.4 2.3 copy-start.11
  144.4 2.3 copy-start.13
  144.4 3.4 copy-start.8
  145.4 157.6 %reduce-scatter.7.cloned.1.call-start = ((), (), s32[]{:S(2)}) async-start(), calls=%async_computation.3 | async-start | bytes 278528 | tf_op jit(solution)/shard_map/reduce_scatter | solution.py:124
  150.7 225.0 %copy-start.1 = (bf16[256,256]{1,0:T(8,128)(2,1)S(1)}, bf16[256,256]{1,0:T(8,128)(2,1)}, u32[]{:S(2)}) copy-start(bf16[256,256]{1,0:T(8,128)(2,1)} %param.16) | copy-start | bytes 393220
Sparse Core Ops, SparseCore 0:
  67.4 81.0 reduce-scatter.10
  152.4 74.1 reduce-scatter.8
  230.6 72.2 reduce-scatter.6
where the time goes:
time: 388 us; the launch traced here: 382 us
  blocking collectives  162 us (42%)
  matrix products  83.6 us (22%)
  waiting for transfers between devices  60.2 us (16%)
  starting transfers between devices  25.7 us (7%)
  local copies, waits for them, and re-layouts  20.9 us (5%)
  between operations  15 us (4%)
  other arithmetic  14.3 us (4%)
    unnamed x1, blocking collectives  89.6 us
    dot_general x54, matrix products, conv_taps(): jnp.dot(window_part, weight[tap_t, tap_h, tap_w], preferred_element_type=...  76 us
    psum x1, blocking collectives, on_device(): lax.psum((adapter_one, adapter_two, kernel_one, kernel_two), 'space')  72.7 us
    reduce_scatter x1, waiting for transfers between devices, on_device(): lax.psum_scatter(summed[0], 'clip', scatter_dimension=0, tiled=True)  56 us
    ppermute x4, starting transfers between devices, padded_2(): lax.ppermute(lax.slice_in_dim(block, block.shape[dim] - width, None, axis...  16.2 us
    ppermute x4, starting transfers between devices, padded_2(): lax.ppermute(lax.slice_in_dim(block, 0, width, axis=dim), axis, backward)  9.42 us
  transfers between devices with their start and end apart: 11, of which 2 were waited for; matrix products, arithmetic and copies ran while one was open for 28% of the time, Pallas kernels for 0%

commit v1 on v0

v1 whole, which is shorter than its diff:
```python
import functools

import jax
import jax.numpy as jnp
from jax import lax
from jax.experimental import pallas as pl
from jax.experimental.pallas import tpu as pltpu
from jax.sharding import PartitionSpec as P

F32 = jnp.float32
BF16 = jnp.bfloat16
MESH = pl.DeviceIdType.MESH
ANY = pl.BlockSpec(memory_space=pl.ANY)
VM = pl.BlockSpec(memory_space=pltpu.VMEM)
VMEM_LIMIT = 60 * 1024 * 1024


def dot(a, b):
    return jnp.dot(a, b, preferred_element_type=F32)


def row_ids(v, width):
    ids = lax.broadcasted_iota(jnp.int32, v.shape, 0)
    return ids if v.shape[0] == width else lax.rem(ids, width)


def from_left(v, width):
    return jnp.where(row_ids(v, width) == 0, 0.0, pltpu.roll(v, 1, 0))


def from_right(v, width):
    return jnp.where(row_ids(v, width) == width - 1, 0.0, pltpu.roll(v, v.shape[0] - 1, 0))


def halo_kernel(x, sl, sh, hx, hl, hh, send_sem, recv_sem):
    me = lax.axis_index("space")
    last = lax.axis_size("space") - 1
    barrier = pltpu.get_barrier_semaphore()

    @pl.when(me > 0)
    def _():
        pl.semaphore_signal(barrier, inc=1, device_id={"space": me - 1}, device_id_type=MESH)

    @pl.when(me < last)
    def _():
        pl.semaphore_signal(barrier, inc=1, device_id={"space": me + 1}, device_id_type=MESH)

    inner = jnp.logical_and(me > 0, me < last)

    @pl.when(inner)
    def _():
        pl.semaphore_wait(barrier, 2)

    @pl.when(jnp.logical_not(inner))
    def _():
        pl.semaphore_wait(barrier, 1)

    def copies(side):
        peer = me + 1 if side == 0 else me - 1
        out = []
        for n, (src, dst, width) in enumerate(((x, hx, 2), (sl, hl, 1), (sh, hh, 1))):
            rows = src.shape[2]
            lo = rows - width if side == 0 else 0
            out.append(
                pltpu.make_async_remote_copy(
                    src_ref=src.at[0, :, lo : lo + width],
                    dst_ref=dst.at[side],
                    send_sem=send_sem.at[side, n],
                    recv_sem=recv_sem.at[side, n],
                    device_id={"space": peer},
                    device_id_type=MESH,
                )
            )
        return out

    down, up = copies(0), copies(1)

    @pl.when(me < last)
    def _():
        for c in down:
            c.start()

    @pl.when(me > 0)
    def _():
        for c in up:
            c.start()

    @pl.when(me < last)
    def _():
        for c in down:
            c.wait_send()
        for c in up:
            c.wait_recv()

    @pl.when(me > 0)
    def _():
        for c in up:
            c.wait_send()
        for c in down:
            c.wait_recv()


def halo_call(x, sl, sh):
    def half(v, width):
        return jax.ShapeDtypeStruct((2, v.shape[1], width) + v.shape[3:], v.dtype)

    return pl.pallas_call(
        halo_kernel,
        out_shape=(half(x, 2), half(sl, 1), half(sh, 1)),
        in_specs=[ANY] * 3,
        out_specs=(ANY,) * 3,
        scratch_shapes=[pltpu.SemaphoreType.DMA((2, 3)), pltpu.SemaphoreType.DMA((2, 3))],
        compiler_params=pltpu.CompilerParams(
            collective_id=0, has_side_effects=True, vmem_limit_bytes=1 << 20
        ),
        name="halo",
    )(x, sl, sh)


def build_taps(w2, v):
    def body(step, _):
        dt, chunk = step // 16, step % 16
        rows = pl.ds(pl.multiple_of(chunk * 16, 16), 16)
        out_rows = pl.ds(pl.multiple_of(dt * 256 + chunk * 16, 16), 16)
        tap = [[w2[dt * 9 + dh * 3 + dw, rows, :].astype(F32) for dw in range(3)] for dh in range(3)]
        for m in range(4):
            r = []
            for dw in range(3):
                a, b, c = tap[0][dw], tap[1][dw], tap[2][dw]
                r.append((a, b + c, a + b, c)[m])
            for j, col in enumerate((r[0], r[1] + r[2], r[0] + r[1], r[2])):
                v[m, out_rows, j * 256 : (j + 1) * 256] = col.astype(BF16)
        return 0

    lax.fori_loop(0, 48, body, 0)


def widen(src, dst):
    for f in range(2):

        def body(r, _):
            dst[f, r] = src[f, r].astype(F32)
            return 0

        lax.fori_loop(0, src.shape[1], body, 0)


def depthwise(u, k, s):
    rows, width = u.shape[1] - 2, u.shape[2]
    for f in range(2):

        def body(r, _):
            parts = [None, None, None]
            for g in range(2):
                for dh in range(3):
                    val = u[g, r + dh]
                    for dw in range(3):
                        tap = (g - f + 1) * 9 + dh * 3 + dw
                        term = val * k[tap : tap + 1, :]
                        parts[dw] = term if parts[dw] is None else parts[dw] + term
            total = u[f, r + 1] + (
                from_left(parts[0], width) + parts[1] + from_right(parts[2], width)
            )
            at = pl.multiple_of((f * rows + r) * width, width)
            s[pl.ds(at, width), :] = total.astype(BF16)
            return 0

        lax.fori_loop(0, rows, body, 0)


def kernel_terms(u, back, kg):
    rows, width, ch = u.shape[1] - 2, u.shape[2], u.shape[3]
    kg[...] = jnp.zeros_like(kg)
    for f in range(2):

        def body(r, _):
            at = pl.multiple_of((f * rows + r) * width, width)
            b = back[pl.ds(at, width), :]
            shifted = (from_right(b, width), b, from_left(b, width))
            for g in range(2):
                for dh in range(3):
                    val = u[g, r + dh]
                    for dw in range(3):
                        tap = (g - f + 1) * 9 + dh * 3 + dw
                        prod = (shifted[dw] * val).reshape(width // 8, 8, ch)
                        kg[tap] += jnp.sum(prod, axis=0)
            return 0

        lax.fori_loop(0, rows, body, 0)


def kernel_rows(kg):
    ch = kg.shape[2]
    summed = jnp.sum(kg[...], axis=1)
    padded = jnp.concatenate([summed, jnp.zeros((128 - 27, ch), F32)], axis=0)
    return padded.T


def local_kernel(
    x, w1, w2, sl, sh, kl, kh, pl_low, pl_high, hx, hl, hh,
    mism, grads,
    xs, w1s, w2s, vs, ys, tgt, gate, ulb, uhb, ul, uh, s_low, s_high, r_low, r_high,
    b_low, b_high, kg_low, kg_high, fine, mism_s, sem, out_sem,
):
    me = lax.axis_index("space")
    last = lax.axis_size("space") - 1
    scale_low = 1.0 / (16 * 2 * 128 * 32)
    scale_high = scale_low / 4

    loads = []

    def load(src, dst):
        c = pltpu.make_async_copy(src, dst, sem.at[len(loads)])
        loads.append(c)
        c.start()
        return c

    c_w2 = load(w2, w2s)
    c_x = [load(x.at[0, f], xs.at[2:10, :, f * 512 : (f + 1) * 512]) for f in range(2)]
    c_sl = load(sl.at[0], ulb.at[:, 1:9])
    c_sh = load(sh.at[0], uhb.at[:, 1:17])
    c_w1 = [
        load(w1.at[dt, :, dw], w1s.at[:, dt * 512 : (dt + 1) * 512, dw * 256 : (dw + 1) * 256])
        for dt in range(3)
        for dw in range(3)
    ]

    def border(side, inside):
        n = 14 + 4 * side
        out = []
        for f in range(2):
            out.append((hx.at[side, f], xs.at[10 * side : 10 * side + 2, :, f * 512 : (f + 1) * 512]))
        out.append((hl.at[side], ulb.at[:, 9 * side : 9 * side + 1]))
        out.append((hh.at[side], uhb.at[:, 17 * side : 17 * side + 1]))

        @pl.when(inside)
        def _():
            cs = [pltpu.make_async_copy(a, b, sem.at[n + q]) for q, (a, b) in enumerate(out)]
            for c in cs:
                c.start()
            for c in cs:
                c.wait()

        @pl.when(jnp.logical_not(inside))
        def _():
            for _, b in out:
                b[...] = jnp.zeros(b.shape, BF16)

    border(0, me > 0)
    border(1, me < last)

    c_w2.wait()
    build_taps(w2s, vs)
    c_sl.wait()
    c_sh.wait()
    widen(ulb, ul)
    widen(uhb, uh)
    depthwise(ul, kl, s_low)
    depthwise(uh, kh, s_high)

    for c in c_x + c_w1:
        c.wait()

    for f in range(2):
        acc = None
        for dh in range(3):
            part = dot(
                xs[dh : dh + 10].reshape(320, 1024), w1s[dh, (1 - f) * 512 : (1 - f) * 512 + 1024, :]
            )
            acc = part if acc is None else acc + part
        ys[:320, :768] = acc
        feat = (
            from_left(ys[:320, 0:256], 32)
            + ys[:320, 256:512]
            + from_right(ys[:320, 512:768], 32)
        ).astype(BF16)
        tgt[f * 256 : (f + 1) * 256, :] = feat[32:288]
        wide = feat.astype(F32)
        gated = wide / (1.0 + jnp.exp(-wide))
        gate[:, :, f * 256 : (f + 1) * 256] = gated.astype(BF16).reshape(10, 32, 256)

    @pl.when(me == 0)
    def _():
        gate[0] = jnp.zeros((32, 512), BF16)

    @pl.when(me == last)
    def _():
        gate[9] = jnp.zeros((32, 512), BF16)

    for q in range(2):
        rows = slice(q * 256, (q + 1) * 256)
        res = dot(s_low[rows, :], pl_low[...]) - tgt[rows, :].astype(F32)
        resid = (res * scale_low).astype(BF16)
        r_low[rows, :] = resid
        b_low[rows, :] = lax.dot_general(
            resid, pl_low[...], (((1,), (1,)), ((), ())), preferred_element_type=F32
        )
    a_low = lax.dot_general(
        s_low[...], r_low[...], (((0,), (0,)), ((), ())), preferred_element_type=F32
    )
    kernel_terms(ul, b_low, kg_low)
    k_low = kernel_rows(kg_low)
    for b in range(16):
        i = (b % 8) * 2 + b // 8
        grads[b * 16 : (b + 1) * 16, 0:256] = a_low[i * 16 : (i + 1) * 16]
        grads[b * 16 : (b + 1) * 16, 256:384] = k_low[i * 16 : (i + 1) * 16]

    for f in range(2):
        for pr in range(2):
            acc = None
            for a in range(2):
                part = dot(
                    gate[pr + a : pr + a + 8].reshape(256, 512),
                    vs[pr * 2 + a, (1 - f) * 256 : (1 - f) * 256 + 512, :],
                )
                acc = part if acc is None else acc + part
            ys[:256, :] = acc
            even = from_left(ys[:256, 0:256], 32) + ys[:256, 256:512]
            odd = ys[:256, 512:768] + from_right(ys[:256, 768:1024], 32)
            for pc, val in enumerate((even, odd)):
                for r in range(8):
                    at = (f * 16 + 2 * r + pr) * 64 + pc
                    for half in range(2):
                        fine[half, pl.ds(at, 32, stride=2), :] = val[
                            r * 32 : (r + 1) * 32, half * 128 : (half + 1) * 128
                        ]

    def fine_body(q, _):
        rows = pl.ds(pl.multiple_of(q * 256, 256), 256)
        target = jnp.concatenate([fine[0, rows, :], fine[1, rows, :]], axis=1)
        target = target.astype(BF16).astype(F32)
        res = dot(s_high[rows, :], pl_high[...]) - target
        mism_s[rows, :] = res.astype(BF16)
        resid = (res * scale_high).astype(BF16)
        r_high[rows, :] = resid
        b_high[rows, :] = lax.dot_general(
            resid, pl_high[...], (((1,), (1,)), ((), ())), preferred_element_type=F32
        )
        return 0

    lax.fori_loop(0, 8, fine_body, 0)
    outs = []
    for f in range(2):
        c = pltpu.make_async_copy(
            mism_s.reshape(2, 16, 64, 256).at[f], mism.at[0, f], out_sem.at[f]
        )
        c.start()
        outs.append(c)
    a_high = lax.dot_general(
        s_high[...], r_high[...], (((0,), (0,)), ((), ())), preferred_element_type=F32
    )
    kernel_terms(uh, b_high, kg_high)
    k_high = kernel_rows(kg_high)
    for b in range(16):
        i = (b % 8) * 2 + b // 8
        grads[b * 16 : b * 16 + 8, 384:512] = a_high[i * 8 : (i + 1) * 8, 0:128]
        grads[b * 16 + 8 : b * 16 + 16, 384:512] = a_high[i * 8 : (i + 1) * 8, 128:256]
        grads[b * 16 : b * 16 + 8, 512:640] = k_high[i * 8 : (i + 1) * 8]
        grads[b * 16 + 8 : b * 16 + 16, 512:640] = jnp.zeros((8, 128), F32)
    for c in outs:
        c.wait()


def local_call(x, w1, w2, sl, sh, kl, kh, p_low, p_high, hx, hl, hh):
    w2 = w2.reshape(27, 256, 256)
    kl = kl.reshape(27, 256)
    kh = kh.reshape(27, 128)
    v = pltpu.VMEM
    return pl.pallas_call(
        local_kernel,
        out_shape=(
            jax.ShapeDtypeStruct((1, 2, 16, 64, 256), BF16),
            jax.ShapeDtypeStruct((256, 640), F32),
        ),
        in_specs=[ANY, ANY, ANY, ANY, ANY, VM, VM, VM, VM, ANY, ANY, ANY],
        out_specs=(ANY, VM),
        scratch_shapes=[
            v((12, 32, 1024), BF16),
            v((3, 1536, 768), BF16),
            v((27, 256, 256), BF16),
            v((4, 768, 1024), BF16),
            v((320, 1024), F32),
            v((512, 256), BF16),
            v((10, 32, 512), BF16),
            v((2, 10, 32, 256), BF16),
            v((2, 18, 64, 128), BF16),
            v((2, 10, 32, 256), F32),
            v((2, 18, 64, 128), F32),
            v((512, 256), BF16),
            v((2048, 128), BF16),
            v((512, 256), BF16),
            v((2048, 256), BF16),
            v((512, 256), F32),
            v((2048, 128), F32),
            v((27, 8, 256), F32),
            v((27, 8, 128), F32),
            v((2, 2048, 128), F32),
            v((2048, 256), BF16),
            pltpu.SemaphoreType.DMA((22,)),
            pltpu.SemaphoreType.DMA((2,)),
        ],
        compiler_params=pltpu.CompilerParams(vmem_limit_bytes=VMEM_LIMIT),
        name="local",
    )(x, w1, w2, sl, sh, kl, kh, p_low, p_high, hx, hl, hh)


def reduce_kernel(
    g, o_al, o_kl, o_ah, o_kh, s1, r1, h1, s2, r2, h2, s3, r3, r4, r5, h3,
    snd, rcv, loc,
):
    clip = lax.axis_index("clip")
    space = lax.axis_index("space")
    core = lax.rem(clip, 2)
    zh = lax.rem(clip // 2, 2)
    y = clip // 4
    zl = space // 4
    xx = lax.rem(space, 4)

    def dev(core=core, y=y, zh=zh, zl=zl, xx=xx):
        return ((y * 2 + zh) * 2 + core, zl * 4 + xx)

    peers = [dev(core=1 - core), dev(zh=1 - zh)]
    for d in range(1, 4):
        peers.append(dev(y=lax.rem(y + d, 4)))
        peers.append(dev(zl=lax.rem(zl + d, 4)))
        peers.append(dev(xx=lax.rem(xx + d, 4)))
    barrier = pltpu.get_barrier_semaphore()
    for p in peers:
        pl.semaphore_signal(barrier, inc=1, device_id=p, device_id_type=MESH)

    s1[...] = g[pl.ds(pl.multiple_of((1 - core) * 128, 128), 128), :].astype(BF16)
    pl.semaphore_wait(barrier, len(peers))

    def send(src, dst, n, peer):
        return pltpu.make_async_remote_copy(
            src_ref=src, dst_ref=dst, send_sem=snd.at[n], recv_sem=rcv.at[n],
            device_id=peer, device_id_type=MESH,
        )

    c = send(s1, r1, 0, dev(core=1 - core))
    c.start()
    c.wait()
    h1[...] = g[pl.ds(pl.multiple_of(core * 128, 128), 128), :] + r1[...].astype(F32)

    s2[...] = h1[...].astype(BF16)
    cs = []
    for d in range(1, 4):
        to = lax.rem(y + d, 4)
        cs.append(
            send(s2.at[pl.ds(pl.multiple_of(to * 32, 32), 32), :], r2.at[d - 1], d, dev(y=to))
        )
    for c in cs:
        c.start()
    for c in cs:
        c.wait()
    h2[...] = h1[pl.ds(pl.multiple_of(y * 32, 32), 32), :] + (
        r2[0].astype(F32) + r2[1].astype(F32) + r2[2].astype(F32)
    )

    s3[...] = h2[...].astype(BF16)
    c = send(s3.at[pl.ds(pl.multiple_of((1 - zh) * 16, 16), 16), :], r3, 4, dev(zh=1 - zh))
    c.start()
    c.wait()
    h3[...] = (h2[pl.ds(pl.multiple_of(zh * 16, 16), 16), :] + r3[...].astype(F32)).astype(BF16)

    def gather(src, slots, mine, base, peer):
        cs = []
        for d in range(1, 4):
            to = lax.rem(mine + d, 4)
            cs.append(send(src, slots.at[mine], base + d, peer(to)))
        for c in cs:
            c.start()
        slots[mine] = src[...]
        for d, c in enumerate(cs):
            c.wait_send()
        for d in range(1, 4):
            came = lax.rem(mine + 4 - d, 4)
            pltpu.make_async_remote_copy(
                src_ref=src, dst_ref=slots.at[came], send_sem=snd.at[base + d],
                recv_sem=rcv.at[base + d], device_id=peer(came), device_id_type=MESH,
            ).wait_recv()
        return (slots[0].astype(F32) + slots[1].astype(F32)) + (
            slots[2].astype(F32) + slots[3].astype(F32)
        )

    total = gather(h3, r4, zl, 4, lambda to: dev(zl=to))
    s3[0:16] = total.astype(BF16)
    total = gather(s3.at[0:16], r5, xx, 7, lambda to: dev(xx=to))
    o_al[...] = total[:, 0:256]
    o_kl[...] = total[:, 256:384]
    o_ah[...] = jnp.concatenate([total[0:8, 384:512], total[8:16, 384:512]], axis=1)
    o_kh[...] = total[0:8, 512:640]


def reduce_call(g):
    v = pltpu.VMEM
    return pl.pallas_call(
        reduce_kernel,
        out_shape=(
            jax.ShapeDtypeStruct((16, 256), F32),
            jax.ShapeDtypeStruct((16, 128), F32),
            jax.ShapeDtypeStruct((8, 256), F32),
            jax.ShapeDtypeStruct((8, 128), F32),
        ),
        in_specs=[VM],
        out_specs=(VM,) * 4,
        scratch_shapes=[
            v((128, 640), BF16),
            v((128, 640), BF16),
            v((128, 640), F32),
            v((128, 640), BF16),
            v((3, 32, 640), BF16),
            v((32, 640), F32),
            v((32, 640), BF16),
            v((16, 640), BF16),
            v((4, 16, 640), BF16),
            v((4, 16, 640), BF16),
            v((16, 640), BF16),
            pltpu.SemaphoreType.DMA((11,)),
            pltpu.SemaphoreType.DMA((11,)),
            pltpu.SemaphoreType.DMA((1,)),
        ],
        compiler_params=pltpu.CompilerParams(
            collective_id=1, has_side_effects=True, vmem_limit_bytes=8 << 20
        ),
        name="reduce",
    )(g)


def on_device(x, w1, w2, sl, sh, kl, kh, p_low, p_high):
    hx, hl, hh = halo_call(x, sl, sh)
    mism, grads = local_call(x, w1, w2, sl, sh, kl, kh, p_low, p_high, hx, hl, hh)
    a_low, k_low, a_high, k_high = reduce_call(grads)
    return (
        a_low,
        k_low[:, :27].T.reshape(3, 3, 3, 16),
        a_high,
        k_high[:, :27].T.reshape(3, 3, 3, 8),
        mism,
    )


def solution(mesh):
    rows = P("clip", None, "space", None, None)
    in_specs = (rows, P(), P(), rows, rows, P(), P(), P(), P())
    out_specs = (
        P("clip", None),
        P(None, None, None, "clip"),
        P("clip", None),
        P(None, None, None, "clip"),
        rows,
    )
    return jax.shard_map(
        on_device, mesh=mesh, in_specs=in_specs, out_specs=out_specs, check_vma=False
    )
```

time: 388 us -> 72.8 us (0.19); the launches traced: 382 us -> 72.4 us
  blocking collectives: 162 us -> 0 us
  matrix products: 83.6 us -> 0 us
  Pallas kernels: 0 us -> 60.3 us
  waiting for transfers between devices: 60.2 us -> 0 us
  starting transfers between devices: 25.7 us -> 0 us
  other arithmetic: 14.3 us -> 0 us
  between operations: 15 us -> 0.7 us
  local copies, waits for them, and re-layouts: 20.9 us -> 11.4 us
    unnamed x1 -> x0, blocking collectives: 89.6 us -> none
    dot_general x60 -> x0, matrix products: 83.6 us -> none  [the longest x54 76 us: conv_taps(): jnp.dot(window_part, weight[tap_t, tap_h, tap_w], preferred_element_type=...]
    psum x1 -> x0, blocking collectives: 72.7 us -> none  [on_device(): lax.psum((adapter_one, adapter_two, kernel_one, kernel_two), 'space')]
    pallas_call x0 -> x3, Pallas kernels: none -> 60.3 us  [the longest x1 27.4 us: reduce_call(): pl.pallas_call(reduce_kernel, out_shape=(jax.ShapeDtypeStruct((16, 256),...]
    reduce_scatter x2 -> x0, waiting for transfers between devices: 56 us -> none  [the longest x1 56 us: on_device(): lax.psum_scatter(summed[0], 'clip', scatter_dimension=0, tiled=True)]
    ppermute x8 -> x0, starting transfers between devices: 25.6 us -> none  [the longest x4 16.2 us: padded_2(): lax.ppermute(lax.slice_in_dim(block, block.shape[dim] - width, None, axis...]
    convert_element_type x4 -> x0, other arithmetic: 9.72 us -> none  [the longest x2 6.79 us: student_level(): student = mixed.astype(jnp.bfloat16)]
    broadcast_in_dim x3 -> x0, local copies, waits for them, and re-layouts: 6.18 us -> none  [the longest x2 6.11 us: on_device(): jnp.repeat(jnp.repeat(gated, 2, axis=2), 2, axis=3)]
  transfers between devices with their start and end apart: 11 -> 0, of which waited for: 2 -> 0; matrix products, arithmetic and copies ran while one was open for 28% -> 0% of each run, Pallas kernels for 0% -> 0%
where the time goes in v1:
time: 72.8 us; the launch traced here: 72.4 us
  Pallas kernels  60.3 us (83%)
  local copies, waits for them, and re-layouts  11.4 us (16%)
    pallas_call x1, Pallas kernels, reduce_call(): pl.pallas_call(reduce_kernel, out_shape=(jax.ShapeDtypeStruct((16, 256),...  27.4 us
    pallas_call x1, Pallas kernels, local_call(): pl.pallas_call(local_kernel, out_shape=(jax.ShapeDtypeStruct((1, 2, 16, 6...  25.5 us
    pallas_call x1, Pallas kernels, halo_call(): pl.pallas_call(halo_kernel, out_shape=(half(x, 2), half(sl, 1), half(sh,...  7.42 us
    unnamed x16, local copies, waits for them, and re-layouts  7.26 us

profile of v1, /device:TPU:2, one launch (start us, length us, event | category | flops | bytes accessed | tf_op | source)
XLA Modules:
  0.0 72.4 jit_solution(14480767941828014494)
XLA Ops:
  0.6 1.3 %reshape.27.kh = f32[27,128]{1,0:T(8,128)} reshape(f32[3,3,3,128]{3,2,1,0:T(4,128)} %param.15) | data formatting | bytes 27648 | tf_op jit(solution)/shard_map/reshape | solution.py:367
  2.0 1.4 %reshape.26.kl = f32[27,256]{1,0:T(8,128)} reshape(f32[3,3,3,256]{3,2,1,0:T(4,128)} %param.14) | data formatting | bytes 55296 | tf_op jit(solution)/shard_map/reshape | solution.py:366
  3.4 0.0 copy-start
  3.4 1.0 %copy-done = bf16[1,2,8,32,512]{4,3,2,1,0:T(8,128)(2,1)S(1)} copy-done((bf16[1,2,8,32,512]{4,3,2,1,0:T(8,128)(2,1)S(1)}, bf16[1,2,8,32,512]{4,3,2,1,0:T(8,128)(2,1)}, u32[]{:S(2)}) %copy-start) | copy-done | bytes 524312
  4.4 0.0 copy-start.1
  4.4 1.0 %copy-done.1 = bf16[1,2,16,64,128]{4,3,2,1,0:T(8,128)(2,1)S(1)} copy-done((bf16[1,2,16,64,128]{4,3,2,1,0:T(8,128)(2,1)S(1)}, bf16[1,2,16,64,128]{4,3,2,1,0:T(8,128)(2,1)}, u32[]{:S(2)}) %copy-start.1) | copy-done | bytes 524312
  5.4 0.0 copy-start.2
  5.4 0.9 %copy-done.2 = bf16[1,2,8,32,256]{4,3,2,1,0:T(8,128)(2,1)S(1)} copy-done((bf16[1,2,8,32,256]{4,3,2,1,0:T(8,128)(2,1)S(1)}, bf16[1,2,8,32,256]{4,3,2,1,0:T(8,128)(2,1)}, u32[]{:S(2)}) %copy-start.2) | copy-done | bytes 262168
  6.4 7.4 %halo.1 = (bf16[2,2,2,32,512]{4,3,2,1,0:T(8,128)(2,1)S(1)}, bf16[2,2,1,32,256]{4,3,2,1,0:T(8,128)(2,1)S(1)}, bf16[2,2,1,64,128]{4,3,2,1,0:T(8,128)(2,1)S(1)}) custom-call(bf16[1,2,8,32,512]{4,3,2,1,0:T(8,128)(2,1)S(1)} %copy-done, bf16[1,2,8,32,256]{4,3,2,1,0:T(8,128)(2,1)S(1)} %copy-done.2, bf16[1,2,16,64,128]{4,3,2,1,0:T(8,128)(2,1)S(1)} %copy-done.1), custom_call_target="tpu_custom_call" | custom-call | tf_op jit(solution)/shard_map/halo/pallas_call | solution.py:107
  13.8 0.0 copy-start.4
  13.8 0.7 copy-done.4
  14.5 0.0 copy-start.5
  14.5 0.6 copy-done.5
  15.2 0.0 copy-start.6
  15.2 0.6 copy-done.6
  15.8 25.5 %local.1 = (bf16[1,2,16,64,256]{4,3,2,1,0:T(8,128)(2,1)}, f32[256,640]{1,0:T(8,128)}) custom-call(bf16[1,2,8,32,512]{4,3,2,1,0:T(8,128)(2,1)} %x.3, bf16[3,3,3,512,256]{4,3,2,1,0:T(8,128)(2,1)} %w1.1, bf16[27,256,256]{2,1,0:T(8,128)(2,1)} %bitcast.5, bf16[1,2,8,32,256]{4,3,2,1,0:T(8,128)(2,1)} %sl.3, bf16[1,2,16,64,128]{4,3,2,1,0:T(8,128)(2,1)} %sh.3, ...), custom_call_target="tpu_custom_call" | custom-call | tf_op jit(solution)/shard_map/local/pallas_call | solution.py:369
  41.3 0.0 copy-start.3
  41.3 1.1 %copy-done.3 = f32[256,640]{1,0:T(8,128)S(1)} copy-done((f32[256,640]{1,0:T(8,128)S(1)}, f32[256,640]{1,0:T(8,128)}, u32[]{:S(2)}) %copy-start.3) | copy-done | bytes 655384
  42.4 27.4 %reduce.1 = (f32[16,256]{1,0:T(8,128)S(1)}, f32[16,128]{1,0:T(8,128)S(1)}, f32[8,256]{1,0:T(8,128)S(1)}, f32[8,128]{1,0:T(8,128)S(1)}) custom-call(f32[256,640]{1,0:T(8,128)S(1)} %copy-done.3), custom_call_target="tpu_custom_call" | custom-call | tf_op jit(solution)/shard_map/reduce/pallas_call | solution.py:497
  69.8 0.1 copy.16
  69.9 0.6 reshape.28
  70.5 0.1 copy.17
  70.6 0.6 reshape.29
  71.2 0.6 copy.20
  71.8 0.6 copy.21
  (2 shorter events, 0.0 us)
Async XLA Ops:
  3.4 1.0 %copy-start = (bf16[1,2,8,32,512]{4,3,2,1,0:T(8,128)(2,1)S(1)}, bf16[1,2,8,32,512]{4,3,2,1,0:T(8,128)(2,1)}, u32[]{:S(2)}) copy-start(bf16[1,2,8,32,512]{4,3,2,1,0:T(8,128)(2,1)} %x.3) | copy-start | bytes 1572868
  4.4 1.0 %copy-start.1 = (bf16[1,2,16,64,128]{4,3,2,1,0:T(8,128)(2,1)S(1)}, bf16[1,2,16,64,128]{4,3,2,1,0:T(8,128)(2,1)}, u32[]{:S(2)}) copy-start(bf16[1,2,16,64,128]{4,3,2,1,0:T(8,128)(2,1)} %sh.3) | copy-start | bytes 1572868
  5.4 0.9 %copy-start.2 = (bf16[1,2,8,32,256]{4,3,2,1,0:T(8,128)(2,1)S(1)}, bf16[1,2,8,32,256]{4,3,2,1,0:T(8,128)(2,1)}, u32[]{:S(2)}) copy-start(bf16[1,2,8,32,256]{4,3,2,1,0:T(8,128)(2,1)} %sl.3) | copy-start | bytes 786436
  13.8 0.7 copy-start.4
  14.5 0.6 copy-start.5
  15.2 0.6 copy-start.6
  41.3 1.1 %copy-start.3 = (f32[256,640]{1,0:T(8,128)S(1)}, f32[256,640]{1,0:T(8,128)}, u32[]{:S(2)}) copy-start(f32[256,640]{1,0:T(8,128)} %get-tuple-element.17.g) | copy-start | bytes 1966084

commit v2 on v1

v2 whole, which is shorter than its diff:
```python
import functools

import jax
import jax.numpy as jnp
from jax import lax
from jax.experimental import pallas as pl
from jax.experimental.pallas import tpu as pltpu
from jax.sharding import PartitionSpec as P

F32 = jnp.float32
BF16 = jnp.bfloat16
MESH = pl.DeviceIdType.MESH
ANY = pl.BlockSpec(memory_space=pl.ANY)
VM = pl.BlockSpec(memory_space=pltpu.VMEM)
VMEM_LIMIT = 60 * 1024 * 1024


def dot(a, b):
    return jnp.dot(a, b, preferred_element_type=F32)


def row_ids(v, width):
    ids = lax.broadcasted_iota(jnp.int32, v.shape, 0)
    return ids if v.shape[0] == width else lax.rem(ids, width)


def from_left(v, width):
    return jnp.where(row_ids(v, width) == 0, 0.0, pltpu.roll(v, 1, 0))


def from_right(v, width):
    return jnp.where(row_ids(v, width) == width - 1, 0.0, pltpu.roll(v, v.shape[0] - 1, 0))


def build_taps(w2, v):
    def body(step, _):
        dt, chunk = step // 16, step % 16
        rows = pl.ds(pl.multiple_of(chunk * 16, 16), 16)
        out_rows = pl.ds(pl.multiple_of(dt * 256 + chunk * 16, 16), 16)
        tap = [[w2[dt, dh, dw, rows, :].astype(F32) for dw in range(3)] for dh in range(3)]
        for m in range(4):
            r = []
            for dw in range(3):
                a, b, c = tap[0][dw], tap[1][dw], tap[2][dw]
                r.append((a, b + c, a + b, c)[m])
            for j, col in enumerate((r[0], r[1] + r[2], r[0] + r[1], r[2])):
                v[m, out_rows, j * 256 : (j + 1) * 256] = col.astype(BF16)
        return 0

    lax.fori_loop(0, 48, body, 0)


def widen(src, dst, first, count):
    for f in range(2):

        def body(r, _):
            dst[f, first + r] = src[f, first + r].astype(F32)
            return 0

        lax.fori_loop(0, count, body, 0)


def depthwise(u, k, s, first, count):
    rows, width = u.shape[1] - 2, u.shape[2]
    for f in range(2):

        def body(step, _):
            r = first + step
            parts = [None, None, None]
            for g in range(2):
                for dh in range(3):
                    val = u[g, r + dh]
                    for dw in range(3):
                        term = val * k[g - f + 1, dh, dw : dw + 1, :]
                        parts[dw] = term if parts[dw] is None else parts[dw] + term
            total = u[f, r + 1] + (
                from_left(parts[0], width) + parts[1] + from_right(parts[2], width)
            )
            at = pl.multiple_of((f * rows + r) * width, width)
            s[pl.ds(at, width), :] = total.astype(BF16)
            return 0

        lax.fori_loop(0, count, body, 0)


def kernel_terms(u, back, kg):
    rows, width, ch = u.shape[1] - 2, u.shape[2], u.shape[3]
    kg[...] = jnp.zeros_like(kg)
    for f in range(2):

        def body(r, _):
            at = pl.multiple_of((f * rows + r) * width, width)
            b = back[pl.ds(at, width), :]
            shifted = (from_right(b, width), b, from_left(b, width))
            for g in range(2):
                for dh in range(3):
                    val = u[g, r + dh]
                    for dw in range(3):
                        tap = (g - f + 1) * 9 + dh * 3 + dw
                        prod = (shifted[dw] * val).reshape(width // 8, 8, ch)
                        kg[tap] += jnp.sum(prod, axis=0)
            return 0

        lax.fori_loop(0, rows, body, 0)


def kernel_rows(kg):
    ch = kg.shape[2]
    summed = jnp.sum(kg[...], axis=1)
    padded = jnp.concatenate([summed, jnp.zeros((128 - 27, ch), F32)], axis=0)
    return padded.T


class Where:
    def __init__(self):
        clip, space = lax.axis_index("clip"), lax.axis_index("space")
        self.space, self.last = space, lax.axis_size("space") - 1
        self.core = lax.rem(clip, 2)
        self.zh = lax.rem(clip // 2, 2)
        self.y = clip // 4
        self.zl = space // 4
        self.x = lax.rem(space, 4)
        self.z = self.zh * 4 + self.zl

    def dev(self, core=None, y=None, z=None, x=None):
        core = self.core if core is None else core
        y = self.y if y is None else y
        zh, zl = (self.zh, self.zl) if z is None else (z // 4, lax.rem(z, 4))
        x = self.x if x is None else x
        return ((y * 2 + zh) * 2 + core, zl * 4 + x)

    def partners(self):
        out = [self.dev(core=1 - self.core)]
        out += [self.dev(y=lax.rem(self.y + d, 4)) for d in range(1, 4)]
        out += [self.dev(z=lax.rem(self.z + d, 8)) for d in range(1, 8)]
        out += [self.dev(x=lax.rem(self.x + d, 4)) for d in range(1, 4)]
        return out


class Reduction:
    def __init__(self, here, g, bufs, snd, rcv):
        self.here, self.g = here, g
        self.s1, self.r1, self.h1, self.s2, self.r2, self.h2, self.r4, self.h4, self.r5 = bufs
        self.snd, self.rcv = snd, rcv

    def copy(self, src, dst, n, peer):
        return pltpu.make_async_remote_copy(
            src_ref=src, dst_ref=dst, send_sem=self.snd.at[n], recv_sem=self.rcv.at[n],
            device_id=peer, device_id_type=MESH,
        )

    def core_start(self):
        t = self.here
        self.s1[...] = self.g[pl.ds(pl.multiple_of((1 - t.core) * 128, 128), 128), :].astype(BF16)
        self.live = [self.copy(self.s1, self.r1, 0, t.dev(core=1 - t.core))]
        self.live[0].start()

    def core_end(self):
        t = self.here
        self.live[0].wait()
        self.h1[...] = self.g[pl.ds(pl.multiple_of(t.core * 128, 128), 128), :] + self.r1[
            ...
        ].astype(F32)

    def y_start(self):
        t = self.here
        self.s2[...] = self.h1[...].astype(BF16)
        self.live = []
        for d in range(1, 4):
            to = lax.rem(t.y + d, 4)
            rows = pl.ds(pl.multiple_of(to * 32, 32), 32)
            self.live.append(self.copy(self.s2.at[rows, :], self.r2.at[d - 1], d, t.dev(y=to)))
        for c in self.live:
            c.start()

    def y_end(self):
        t = self.here
        for c in self.live:
            c.wait()
        r2 = self.r2
        self.h2[...] = (
            self.h1[pl.ds(pl.multiple_of(t.y * 32, 32), 32), :]
            + (r2[0].astype(F32) + r2[1].astype(F32) + r2[2].astype(F32))
        ).astype(BF16)

    def share_start(self, source, slots, mine, size, base, peer):
        cs = []
        for d in range(1, size):
            to = lax.rem(mine + d, size)
            cs.append(self.copy(source(to), slots.at[mine], base + d, peer(to)))
        for c in cs:
            c.start()
        slots[mine] = source(mine)[...]
        self.live = cs

    def share_end(self, source, slots, mine, size, base, peer):
        for c in self.live:
            c.wait_send()
        for d in range(1, size):
            came = lax.rem(mine + size - d, size)
            self.copy(source(came), slots.at[came], base + d, peer(came)).wait_recv()
        vals = [slots[n].astype(F32) for n in range(size)]
        while len(vals) > 1:
            vals = [vals[n] + vals[n + 1] for n in range(0, len(vals), 2)]
        return vals[0]

    def z_args(self):
        t = self.here
        source = lambda z: self.h2.at[pl.ds(pl.multiple_of(z // 4 * 16, 16), 16), :]
        return source, self.r4, t.z, 8, 3, lambda z: t.dev(z=z)

    def x_args(self):
        t = self.here
        return lambda x: self.h4, self.r5, t.x, 4, 10, lambda x: t.dev(x=x)

    def z_start(self):
        self.share_start(*self.z_args())

    def z_end(self):
        self.h4[...] = self.share_end(*self.z_args()).astype(BF16)

    def x_start(self):
        self.share_start(*self.x_args())

    def x_end(self):
        return self.share_end(*self.x_args())


def step_kernel(
    x, w1, w2, sl, sh, kl_in, kh_in, al_in, ah_in,
    mism, o_al, o_kl, o_ah, o_kh,
    xs, w1s, w2s, vs, ys, tgt, fh, gate, kl, kh, p_low, p_high,
    ulb, uhb, ul, uh, s_low, s_high, r_low, r_high,
    b_low, b_high, kg_low, kg_high, fine, mism_s, g_low, g_high,
    *rest,
):
    bufs_low, bufs_high = rest[:9], rest[9:18]
    sem, out_sem, halo_snd, halo_rcv, snd_low, rcv_low, snd_high, rcv_high = rest[18:]
    here = Where()
    me, last = here.space, here.last
    scale_low = 1.0 / (16 * 2 * 128 * 32)
    scale_high = scale_low / 4

    barrier = pltpu.get_barrier_semaphore()
    partners = here.partners()
    for p in partners:
        pl.semaphore_signal(barrier, inc=1, device_id=p, device_id_type=MESH)

    @pl.when(me > 0)
    def _():
        pl.semaphore_signal(barrier, inc=1, device_id={"space": me - 1}, device_id_type=MESH)

    @pl.when(me < last)
    def _():
        pl.semaphore_signal(barrier, inc=1, device_id={"space": me + 1}, device_id_type=MESH)

    loads = []

    def load(src, dst):
        c = pltpu.make_async_copy(src, dst, sem.at[len(loads)])
        loads.append(c)
        c.start()
        return c

    c_w2 = load(w2, w2s)
    c_sl = load(sl.at[0], ulb.at[:, 1:9])
    c_sh = load(sh.at[0], uhb.at[:, 1:17])
    c_k = [load(kl_in, kl), load(kh_in, kh), load(al_in, p_low), load(ah_in, p_high)]
    c_x = [load(x.at[0, f], xs.at[1:9, :, f * 512 : (f + 1) * 512]) for f in range(2)]
    c_w1 = [
        load(w1.at[dt, :, dw], w1s.at[:, dt * 512 : (dt + 1) * 512, dw * 256 : (dw + 1) * 256])
        for dt in range(3)
        for dw in range(3)
    ]

    c_w2.wait()
    build_taps(w2s, vs)

    inner = jnp.logical_and(me > 0, me < last)

    @pl.when(inner)
    def _():
        pl.semaphore_wait(barrier, len(partners) + 2)

    @pl.when(jnp.logical_not(inner))
    def _():
        pl.semaphore_wait(barrier, len(partners) + 1)

    def border(side):
        peer = me + 1 if side == 0 else me - 1
        row, low, high = (7, 0, 0) if side == 0 else (0, 9, 17)
        fine_row = 15 if side == 0 else 0
        pairs = [
            (x.at[0, f, row : row + 1], xs.at[low : low + 1, :, f * 512 : (f + 1) * 512])
            for f in range(2)
        ]
        pairs.append((sh.at[0, :, fine_row : fine_row + 1], uhb.at[:, high : high + 1]))
        pairs.append((sl.at[0, :, row : row + 1], ulb.at[:, low : low + 1]))
        pairs.append((tgt.at[:, row * 32 : (row + 1) * 32], fh.at[side]))
        return [
            pltpu.make_async_remote_copy(
                src_ref=a, dst_ref=b, send_sem=halo_snd.at[side, n], recv_sem=halo_rcv.at[side, n],
                device_id={"space": peer}, device_id_type=MESH,
            )
            for n, (a, b) in enumerate(pairs)
        ]

    down, up = border(0), border(1)

    @pl.when(me < last)
    def _():
        for c in down[:4]:
            c.start()

    @pl.when(me > 0)
    def _():
        for c in up[:4]:
            c.start()

    c_sl.wait()
    c_sh.wait()
    for c in c_k:
        c.wait()
    widen(ulb, ul, 1, 8)
    widen(uhb, uh, 1, 16)
    depthwise(ul, kl, s_low, 1, 6)
    depthwise(uh, kh, s_high, 1, 14)

    for c in c_x + c_w1:
        c.wait()

    @pl.when(me > 0)
    def _():
        for c in down[:2]:
            c.wait_recv()

    @pl.when(me == 0)
    def _():
        xs[0] = jnp.zeros((32, 1024), BF16)

    @pl.when(me < last)
    def _():
        for c in up[:2]:
            c.wait_recv()

    @pl.when(me == last)
    def _():
        xs[9] = jnp.zeros((32, 1024), BF16)

    for f in range(2):
        acc = None
        for dh in range(3):
            part = dot(
                xs[dh : dh + 8].reshape(256, 1024), w1s[dh, (1 - f) * 512 : (1 - f) * 512 + 1024, :]
            )
            acc = part if acc is None else acc + part
        ys[:, :768] = acc
        tgt[f] = (
            from_left(ys[:, 0:256], 32) + ys[:, 256:512] + from_right(ys[:, 512:768], 32)
        ).astype(BF16)

    @pl.when(me < last)
    def _():
        down[4].start()

    @pl.when(me > 0)
    def _():
        up[4].start()

    def gated(v):
        wide = v.astype(F32)
        return (wide / (1.0 + jnp.exp(-wide))).astype(BF16)

    for f in range(2):
        gate[1:9, :, f * 256 : (f + 1) * 256] = gated(tgt[f]).reshape(8, 32, 256)

    @pl.when(me > 0)
    def _():
        for c in down[2:4]:
            c.wait_recv()

    @pl.when(me == 0)
    def _():
        for f in range(2):
            ulb[f, 0] = jnp.zeros((32, 256), BF16)
            uhb[f, 0] = jnp.zeros((64, 128), BF16)

    @pl.when(me < last)
    def _():
        for c in up[2:4]:
            c.wait_recv()

    @pl.when(me == last)
    def _():
        for f in range(2):
            ulb[f, 9] = jnp.zeros((32, 256), BF16)
            uhb[f, 17] = jnp.zeros((64, 128), BF16)

    for first in (0, 9):
        widen(ulb, ul, first, 1)
    for first in (0, 17):
        widen(uhb, uh, first, 1)
    for first in (0, 7):
        depthwise(ul, kl, s_low, first, 1)
    for first in (0, 15):
        depthwise(uh, kh, s_high, first, 1)

    for f in range(2):
        rows = slice(f * 256, (f + 1) * 256)
        res = dot(s_low[rows, :], p_low[...]) - tgt[f].astype(F32)
        resid = (res * scale_low).astype(BF16)
        r_low[rows, :] = resid
        b_low[rows, :] = lax.dot_general(
            resid, p_low[...], (((1,), (1,)), ((), ())), preferred_element_type=F32
        )
    a_low = lax.dot_general(
        s_low[...], r_low[...], (((0,), (0,)), ((), ())), preferred_element_type=F32
    )
    kernel_terms(ul, b_low, kg_low)
    k_low = kernel_rows(kg_low)
    for b in range(16):
        i = (b % 8) * 2 + b // 8
        g_low[b * 16 : (b + 1) * 16, 0:256] = a_low[i * 16 : (i + 1) * 16]
        g_low[b * 16 : (b + 1) * 16, 256:384] = k_low[i * 16 : (i + 1) * 16]
    red_low = Reduction(here, g_low, bufs_low, snd_low, rcv_low)
    red_low.core_start()

    @pl.when(me > 0)
    def _():
        down[4].wait_recv()
        for f in range(2):
            gate[0, :, f * 256 : (f + 1) * 256] = gated(fh[0, f])

    @pl.when(me == 0)
    def _():
        gate[0] = jnp.zeros((32, 512), BF16)

    @pl.when(me < last)
    def _():
        up[4].wait_recv()
        for f in range(2):
            gate[9, :, f * 256 : (f + 1) * 256] = gated(fh[1, f])

    @pl.when(me == last)
    def _():
        gate[9] = jnp.zeros((32, 512), BF16)

    for f in range(2):
        for pr in range(2):
            acc = None
            for a in range(2):
                part = dot(
                    gate[pr + a : pr + a + 8].reshape(256, 512),
                    vs[pr * 2 + a, (1 - f) * 256 : (1 - f) * 256 + 512, :],
                )
                acc = part if acc is None else acc + part
            ys[...] = acc
            even = from_left(ys[:, 0:256], 32) + ys[:, 256:512]
            odd = ys[:, 512:768] + from_right(ys[:, 768:1024], 32)
            for pc, val in enumerate((even, odd)):
                for r in range(8):
                    at = (f * 16 + 2 * r + pr) * 64 + pc
                    for half in range(2):
                        fine[half, pl.ds(at, 32, stride=2), :] = val[
                            r * 32 : (r + 1) * 32, half * 128 : (half + 1) * 128
                        ]
        if f == 0:
            red_low.core_end()
            red_low.y_start()
        else:
            red_low.y_end()
            red_low.z_start()

    def fine_body(q, _):
        rows = pl.ds(pl.multiple_of(q * 256, 256), 256)
        target = jnp.concatenate([fine[0, rows, :], fine[1, rows, :]], axis=1)
        target = target.astype(BF16).astype(F32)
        res = dot(s_high[rows, :], p_high[...]) - target
        mism_s[rows, :] = res.astype(BF16)
        resid = (res * scale_high).astype(BF16)
        r_high[rows, :] = resid
        b_high[rows, :] = lax.dot_general(
            resid, p_high[...], (((1,), (1,)), ((), ())), preferred_element_type=F32
        )
        return 0

    lax.fori_loop(0, 8, fine_body, 0)
    outs = []
    for f in range(2):
        c = pltpu.make_async_copy(
            mism_s.reshape(2, 16, 64, 256).at[f], mism.at[0, f], out_sem.at[f]
        )
        c.start()
        outs.append(c)
    red_low.z_end()
    red_low.x_start()
    a_high = lax.dot_general(
        s_high[...], r_high[...], (((0,), (0,)), ((), ())), preferred_element_type=F32
    )
    kernel_terms(uh, b_high, kg_high)
    k_high = kernel_rows(kg_high)
    for b in range(16):
        i = (b % 8) * 2 + b // 8
        g_high[b * 16 : b * 16 + 8, 0:128] = a_high[i * 8 : (i + 1) * 8, 0:128]
        g_high[b * 16 + 8 : b * 16 + 16, 0:128] = a_high[i * 8 : (i + 1) * 8, 128:256]
        g_high[b * 16 : b * 16 + 8, 128:256] = k_high[i * 8 : (i + 1) * 8]
        g_high[b * 16 + 8 : b * 16 + 16, 128:256] = jnp.zeros((8, 128), F32)
    red_high = Reduction(here, g_high, bufs_high, snd_high, rcv_high)
    red_high.core_start()
    low = red_low.x_end()
    o_al[...] = low[:, 0:256]
    low_k = jnp.concatenate([low[:, 256:384], jnp.zeros((112, 128), F32)], axis=0).T
    for dt in range(3):
        for dh in range(3):
            n = (dt * 3 + dh) * 3
            o_kl[dt, dh] = low_k[n : n + 3, 0:16]
    red_high.core_end()
    red_high.y_start()
    red_high.y_end()
    red_high.z_start()
    red_high.z_end()
    red_high.x_start()
    high = red_high.x_end()
    o_ah[...] = jnp.concatenate([high[0:8, 0:128], high[8:16, 0:128]], axis=1)
    high_k = jnp.concatenate([high[0:8, 128:256], jnp.zeros((120, 128), F32)], axis=0).T
    for dt in range(3):
        for dh in range(3):
            n = (dt * 3 + dh) * 3
            o_kh[dt, dh] = high_k[n : n + 3, 0:8]

    for c in outs:
        c.wait()

    @pl.when(me < last)
    def _():
        for c in down:
            c.wait_send()

    @pl.when(me > 0)
    def _():
        for c in up:
            c.wait_send()


def step_call(x, w1, w2, sl, sh, kl, kh, p_low, p_high):
    v = pltpu.VMEM
    dma = pltpu.SemaphoreType.DMA

    def reduction_buffers(lanes):
        return [
            v((128, lanes), BF16),
            v((128, lanes), BF16),
            v((128, lanes), F32),
            v((128, lanes), BF16),
            v((3, 32, lanes), BF16),
            v((32, lanes), BF16),
            v((8, 16, lanes), BF16),
            v((16, lanes), BF16),
            v((4, 16, lanes), BF16),
        ]

    return pl.pallas_call(
        step_kernel,
        out_shape=(
            jax.ShapeDtypeStruct((1, 2, 16, 64, 256), BF16),
            jax.ShapeDtypeStruct((16, 256), F32),
            jax.ShapeDtypeStruct((3, 3, 3, 16), F32),
            jax.ShapeDtypeStruct((8, 256), F32),
            jax.ShapeDtypeStruct((3, 3, 3, 8), F32),
        ),
        in_specs=[ANY] * 9,
        out_specs=(ANY, VM, VM, VM, VM),
        scratch_shapes=[
            v((10, 32, 1024), BF16),
            v((3, 1536, 768), BF16),
            v((3, 3, 3, 256, 256), BF16),
            v((4, 768, 1024), BF16),
            v((256, 1024), F32),
            v((2, 256, 256), BF16),
            v((2, 2, 32, 256), BF16),
            v((10, 32, 512), BF16),
            v((3, 3, 3, 256), F32),
            v((3, 3, 3, 128), F32),
            v((256, 256), BF16),
            v((128, 256), BF16),
            v((2, 10, 32, 256), BF16),
            v((2, 18, 64, 128), BF16),
            v((2, 10, 32, 256), F32),
            v((2, 18, 64, 128), F32),
            v((512, 256), BF16),
            v((2048, 128), BF16),
            v((512, 256), BF16),
            v((2048, 256), BF16),
            v((512, 256), F32),
            v((2048, 128), F32),
            v((27, 8, 256), F32),
            v((27, 8, 128), F32),
            v((2, 2048, 128), F32),
            v((2048, 256), BF16),
            v((256, 384), F32),
            v((256, 256), F32),
            *reduction_buffers(384),
            *reduction_buffers(256),
            dma((18,)),
            dma((2,)),
            dma((2, 5)),
            dma((2, 5)),
            dma((14,)),
            dma((14,)),
            dma((14,)),
            dma((14,)),
        ],
        compiler_params=pltpu.CompilerParams(
            collective_id=0, has_side_effects=True, vmem_limit_bytes=VMEM_LIMIT
        ),
        name="step",
    )(x, w1, w2, sl, sh, kl, kh, p_low, p_high)


def on_device(*args):
    mism, a_low, k_low, a_high, k_high = step_call(*args)
    return a_low, k_low, a_high, k_high, mism


def solution(mesh):
    rows = P("clip", None, "space", None, None)
    in_specs = (rows, P(), P(), rows, rows, P(), P(), P(), P())
    out_specs = (
        P("clip", None),
        P(None, None, None, "clip"),
        P("clip", None),
        P(None, None, None, "clip"),
        rows,
    )
    return jax.shard_map(
        on_device, mesh=mesh, in_specs=in_specs, out_specs=out_specs, check_vma=False
    )
```

time: 72.8 us -> 57.7 us (0.79)
  Pallas kernels: 60.3 us -> 49 us
  local copies, waits for them, and re-layouts: 11.4 us -> 7.58 us
    pallas_call x3 -> x1, Pallas kernels: 60.3 us -> 49 us  [step_call(): pl.pallas_call(step_kernel, out_shape=(jax.ShapeDtypeStruct((1, 2, 16, 64...]
    reshape x4 -> x0, local copies, waits for them, and re-layouts: 3.96 us -> none  [the longest x1 1.39 us: local_call(): kl = kl.reshape(27, 256)]
    unnamed x16 -> x5, local copies, waits for them, and re-layouts: 7.26 us -> 7.58 us
where the time goes in v2:
time: 57.7 us; the launch traced here: 57.2 us
  Pallas kernels  49 us (85%)
  local copies, waits for them, and re-layouts  7.58 us (13%)
  between operations  0.64 us (1%)
    pallas_call x1, Pallas kernels, step_call(): pl.pallas_call(step_kernel, out_shape=(jax.ShapeDtypeStruct((1, 2, 16, 64...  49 us
    unnamed x5, local copies, waits for them, and re-layouts  7.58 us

profile of v2, /device:TPU:2, one launch (start us, length us, event | category | flops | bytes accessed | tf_op | source)
XLA Modules:
  0.0 57.2 jit_solution(7145847306094294370)
XLA Ops:
  0.6 49.0 %step.1 = (bf16[1,2,16,64,256]{4,3,2,1,0:T(8,128)(2,1)}, f32[16,256]{1,0:T(8,128)}, f32[3,3,3,16]{3,2,1,0:T(4,128)}, f32[8,256]{1,0:T(8,128)}, f32[3,3,3,8]{3,2,1,0:T(4,128)}) custom-call(bf16[1,2,8,32,512]{4,3,2,1,0:T(8,128)(2,1)} %x.1, bf16[3,3,3,512,256]{4,3,2,1,0:T(8,128)(2,1)} %w1.1, bf16[3,3,3,256,256]{4,3,2,1,0:T(8,128)(2,1)} %w2.1, ...), custom_call_target="tpu_custom_call" | custom-call | tf_op jit(solution)/shard_map/step/pallas_call | solution.py:562
  49.7 1.3 %copy.19 = f32[16,256]{1,0:T(8,128)} copy(f32[16,256]{1,0:T(8,128)} %get-tuple-element.20) | data formatting | bytes 32768
  51.0 1.3 %copy.20 = f32[3,3,3,16]{3,2,1,0:T(4,128)} copy(f32[3,3,3,16]{3,2,1,0:T(4,128)} %get-tuple-element.21) | data formatting | bytes 3456
  52.3 1.3 %copy.21 = f32[8,256]{1,0:T(8,128)} copy(f32[8,256]{1,0:T(8,128)} %get-tuple-element.22) | data formatting | bytes 16384
  53.6 1.3 %copy.22 = f32[3,3,3,8]{3,2,1,0:T(4,128)} copy(f32[3,3,3,8]{3,2,1,0:T(4,128)} %get-tuple-element.23) | data formatting | bytes 1728
  54.9 2.3 %copy.23 = bf16[1,2,16,64,256]{4,3,2,1,0:T(8,128)(2,1)} copy(bf16[1,2,16,64,256]{4,3,2,1,0:T(8,128)(2,1)} %get-tuple-element.24) | data formatting | bytes 2097152

commit v3 on v2

--- a/solution.py
+++ b/solution.py
@@ -11,8 +11,9 @@
 BF16 = jnp.bfloat16
 MESH = pl.DeviceIdType.MESH
 ANY = pl.BlockSpec(memory_space=pl.ANY)
+HBM = pl.BlockSpec(memory_space=pltpu.HBM)
 VM = pl.BlockSpec(memory_space=pltpu.VMEM)
-VMEM_LIMIT = 60 * 1024 * 1024
+STEP_VMEM = 40 * 1024 * 1024
 
 
 def dot(a, b):
@@ -228,14 +229,14 @@
 
 def step_kernel(
     x, w1, w2, sl, sh, kl_in, kh_in, al_in, ah_in,
-    mism, o_al, o_kl, o_ah, o_kh,
+    mism_s, o_low, o_high,
     xs, w1s, w2s, vs, ys, tgt, fh, gate, kl, kh, p_low, p_high,
     ulb, uhb, ul, uh, s_low, s_high, r_low, r_high,
-    b_low, b_high, kg_low, kg_high, fine, mism_s, g_low, g_high,
+    b_low, b_high, kg_low, kg_high, fine, g_low, g_high,
     *rest,
 ):
     bufs_low, bufs_high = rest[:9], rest[9:18]
-    sem, out_sem, halo_snd, halo_rcv, snd_low, rcv_low, snd_high, rcv_high = rest[18:]
+    sem, halo_snd, halo_rcv, snd_low, rcv_low, snd_high, rcv_high = rest[18:]
     here = Where()
     me, last = here.space, here.last
     scale_low = 1.0 / (16 * 2 * 128 * 32)
@@ -485,13 +486,6 @@
         return 0
 
     lax.fori_loop(0, 8, fine_body, 0)
-    outs = []
-    for f in range(2):
-        c = pltpu.make_async_copy(
-            mism_s.reshape(2, 16, 64, 256).at[f], mism.at[0, f], out_sem.at[f]
-        )
-        c.start()
-        outs.append(c)
     red_low.z_end()
     red_low.x_start()
     a_high = lax.dot_general(
@@ -507,29 +501,14 @@
         g_high[b * 16 + 8 : b * 16 + 16, 128:256] = jnp.zeros((8, 128), F32)
     red_high = Reduction(here, g_high, bufs_high, snd_high, rcv_high)
     red_high.core_start()
-    low = red_low.x_end()
-    o_al[...] = low[:, 0:256]
-    low_k = jnp.concatenate([low[:, 256:384], jnp.zeros((112, 128), F32)], axis=0).T
-    for dt in range(3):
-        for dh in range(3):
-            n = (dt * 3 + dh) * 3
-            o_kl[dt, dh] = low_k[n : n + 3, 0:16]
+    o_low[...] = red_low.x_end()
     red_high.core_end()
     red_high.y_start()
     red_high.y_end()
     red_high.z_start()
     red_high.z_end()
     red_high.x_start()
-    high = red_high.x_end()
-    o_ah[...] = jnp.concatenate([high[0:8, 0:128], high[8:16, 0:128]], axis=1)
-    high_k = jnp.concatenate([high[0:8, 128:256], jnp.zeros((120, 128), F32)], axis=0).T
-    for dt in range(3):
-        for dh in range(3):
-            n = (dt * 3 + dh) * 3
-            o_kh[dt, dh] = high_k[n : n + 3, 0:8]
-
-    for c in outs:
-        c.wait()
+    o_high[...] = red_high.x_end()
 
     @pl.when(me < last)
     def _():
@@ -562,14 +541,12 @@
     return pl.pallas_call(
         step_kernel,
         out_shape=(
-            jax.ShapeDtypeStruct((1, 2, 16, 64, 256), BF16),
+            jax.ShapeDtypeStruct((2048, 256), BF16),
+            jax.ShapeDtypeStruct((16, 384), F32),
             jax.ShapeDtypeStruct((16, 256), F32),
-            jax.ShapeDtypeStruct((3, 3, 3, 16), F32),
-            jax.ShapeDtypeStruct((8, 256), F32),
-            jax.ShapeDtypeStruct((3, 3, 3, 8), F32),
         ),
-        in_specs=[ANY] * 9,
-        out_specs=(ANY, VM, VM, VM, VM),
+        in_specs=[HBM] * 9,
+        out_specs=(VM, VM, VM),
         scratch_shapes=[
             v((10, 32, 1024), BF16),
             v((3, 1536, 768), BF16),
@@ -596,13 +573,11 @@
             v((27, 8, 256), F32),
             v((27, 8, 128), F32),
             v((2, 2048, 128), F32),
-            v((2048, 256), BF16),
             v((256, 384), F32),
             v((256, 256), F32),
             *reduction_buffers(384),
             *reduction_buffers(256),
             dma((18,)),
-            dma((2,)),
             dma((2, 5)),
             dma((2, 5)),
             dma((14,)),
@@ -611,14 +586,50 @@
             dma((14,)),
         ],
         compiler_params=pltpu.CompilerParams(
-            collective_id=0, has_side_effects=True, vmem_limit_bytes=VMEM_LIMIT
+            collective_id=0, has_side_effects=True, vmem_limit_bytes=STEP_VMEM
         ),
         name="step",
-    )(x, w1, w2, sl, sh, kl, kh, p_low, p_high)
+    )(*(pltpu.with_memory_space_constraint(v, pltpu.HBM) for v in (x, w1, w2, sl, sh, kl, kh, p_low, p_high)))
+
+
+def unpack_kernel(mism_s, low, high, mism, o_al, o_kl, o_ah, o_kh, sem):
+    cs = [
+        pltpu.make_async_copy(
+            mism_s.reshape(2, 16, 64, 256).at[f], mism.at[0, f], sem.at[f]
+        )
+        for f in range(2)
+    ]
+    for c in cs:
+        c.start()
+    o_al[...] = low[:, 0:256]
+    o_ah[...] = jnp.concatenate([high[0:8, 0:128], high[8:16, 0:128]], axis=1)
+    low_k = jnp.concatenate([low[:, 256:384], jnp.zeros((112, 128), F32)], axis=0).T
+    high_k = jnp.concatenate([high[0:8, 128:256], jnp.zeros((120, 128), F32)], axis=0).T
+    for dt in range(3):
+        for dh in range(3):
+            n = (dt * 3 + dh) * 3
+            o_kl[dt, dh] = low_k[n : n + 3, 0:16]
+            o_kh[dt, dh] = high_k[n : n + 3, 0:8]
+    for c in cs:
+        c.wait()
 
 
 def on_device(*args):
-    mism, a_low, k_low, a_high, k_high = step_call(*args)
+    mism, a_low, k_low, a_high, k_high = pl.pallas_call(
+        unpack_kernel,
+        out_shape=(
+            jax.ShapeDtypeStruct((1, 2, 16, 64, 256), BF16),
+            jax.ShapeDtypeStruct((16, 256), F32),
+            jax.ShapeDtypeStruct((3, 3, 3, 16), F32),
+            jax.ShapeDtypeStruct((8, 256), F32),
+            jax.ShapeDtypeStruct((3, 3, 3, 8), F32),
+        ),
+        in_specs=[VM] * 3,
+        out_specs=(HBM, VM, VM, VM, VM),
+        scratch_shapes=[pltpu.SemaphoreType.DMA((2,))],
+        compiler_params=pltpu.CompilerParams(vmem_limit_bytes=4 << 20),
+        name="unpack",
+    )(*step_call(*args))
     return a_low, k_low, a_high, k_high, mism
 
 

time: 57.7 us -> 50.7 us (0.88)
  local copies, waits for them, and re-layouts: 7.58 us -> 0 us
  Pallas kernels: 49 us -> 49.9 us
    unnamed x5 -> x0, local copies, waits for them, and re-layouts: 7.58 us -> none
    pallas_call x1 -> x2, Pallas kernels: 49 us -> 49.9 us  [the longest x1 48.3 us: step_call(): pl.pallas_call(step_kernel, out_shape=(jax.ShapeDtypeStruct((2048, 256),...]
where the time goes in v3:
time: 50.7 us; the launch traced here: 50.5 us
  Pallas kernels  49.9 us (98%)
  between operations  0.64 us (1%)
    pallas_call x1, Pallas kernels, step_call(): pl.pallas_call(step_kernel, out_shape=(jax.ShapeDtypeStruct((2048, 256),...  48.3 us
    pallas_call x1, Pallas kernels, on_device(): pl.pallas_call(unpack_kernel, out_shape=(jax.ShapeDtypeStruct((1, 2, 16,...  1.61 us

profile of v3, /device:TPU:2, one launch (start us, length us, event | category | flops | bytes accessed | tf_op | source)
XLA Modules:
  0.0 50.5 jit_solution(8148846187984339531)
XLA Ops:
  0.6 48.3 %step.1 = (bf16[2048,256]{1,0:T(8,128)(2,1)S(1)}, f32[16,384]{1,0:T(8,128)S(1)}, f32[16,256]{1,0:T(8,128)S(1)}) custom-call(bf16[1,2,8,32,512]{4,3,2,1,0:T(8,128)(2,1)} %x.1, bf16[3,3,3,512,256]{4,3,2,1,0:T(8,128)(2,1)} %w1.1, bf16[3,3,3,256,256]{4,3,2,1,0:T(8,128)(2,1)} %w2.1, bf16[1,2,8,32,256]{4,3,2,1,0:T(8,128)(2,1)} %sl.1, ...), custom_call_target="tpu_custom_call" | custom-call | tf_op jit(solution)/shard_map/step/pallas_call | solution.py:541
  48.9 1.6 %unpack.1 = (bf16[1,2,16,64,256]{4,3,2,1,0:T(8,128)(2,1)}, f32[16,256]{1,0:T(8,128)}, f32[3,3,3,16]{3,2,1,0:T(4,128)}, f32[8,256]{1,0:T(8,128)}, f32[3,3,3,8]{3,2,1,0:T(4,128)}) custom-call(bf16[2048,256]{1,0:T(8,128)(2,1)S(1)} %get-tuple-element.13.mism_s, f32[16,384]{1,0:T(8,128)S(1)} %get-tuple-element.14.low, f32[16,256]{1,0:T(8,128)S(1)} %get-tuple-element.15.high), custom_call_target="tpu_custom_call" | custom-call | tf_op jit(solution)/shard_map/unpack/pallas_call | solution.py:618

commit v4 on v3

--- a/solution.py
+++ b/solution.py
@@ -45,7 +45,7 @@
                 a, b, c = tap[0][dw], tap[1][dw], tap[2][dw]
                 r.append((a, b + c, a + b, c)[m])
             for j, col in enumerate((r[0], r[1] + r[2], r[0] + r[1], r[2])):
-                v[m, out_rows, j * 256 : (j + 1) * 256] = col.astype(BF16)
+                v[m, out_rows, j * 256 : (j + 1) * 256] = (-col).astype(BF16)
         return 0
 
     lax.fori_loop(0, 48, body, 0)
@@ -84,6 +84,63 @@
         lax.fori_loop(0, count, body, 0)
 
 
+def widen_fine(src, tmp, dst, first, count):
+    for f in range(2):
+
+        def body(step, _):
+            r = first + step
+            tmp[...] = src[f, r].astype(F32)
+            for pc in range(2):
+                dst[pc, f, r] = tmp[pl.ds(pc, 32, stride=2), :]
+            return 0
+
+        lax.fori_loop(0, count, body, 0)
+
+
+def fine_rows(f, r, pc):
+    return pl.ds(pl.multiple_of((f * 4 + lax.rem(r, 2) * 2 + pc) * 256 + r // 2 * 32, 32), 32)
+
+
+def depthwise_fine(u, k, s, first, count):
+    for f in range(2):
+
+        def body(step, _):
+            r = first + step
+            left = even = odd = right = 0.0
+            for g in range(2):
+                for dh in range(3):
+                    e, o = u[0, g, r + dh], u[1, g, r + dh]
+                    k0, k1, k2 = (k[g - f + 1, dh, dw : dw + 1, :] for dw in range(3))
+                    left += o * k0
+                    even += e * k1 + o * k2
+                    odd += e * k0 + o * k1
+                    right += e * k2
+            s[fine_rows(f, r, 0), :] = (u[0, f, r + 1] + (from_left(left, 32) + even)).astype(BF16)
+            s[fine_rows(f, r, 1), :] = (u[1, f, r + 1] + (odd + from_right(right, 32))).astype(BF16)
+            return 0
+
+        lax.fori_loop(0, count, body, 0)
+
+
+def kernel_terms_fine(u, back, kg):
+    kg[...] = jnp.zeros_like(kg)
+    for f in range(2):
+
+        def body(r, _):
+            be, bo = back[fine_rows(f, r, 0), :], back[fine_rows(f, r, 1), :]
+            be_right, bo_left = from_right(be, 32), from_left(bo, 32)
+            for g in range(2):
+                for dh in range(3):
+                    e, o = u[0, g, r + dh], u[1, g, r + dh]
+                    terms = (be_right * o + bo * e, be * e + bo * o, be * o + bo_left * e)
+                    for dw in range(3):
+                        tap = (g - f + 1) * 9 + dh * 3 + dw
+                        kg[tap] += jnp.sum(terms[dw].reshape(4, 8, 128), axis=0)
+            return 0
+
+        lax.fori_loop(0, 16, body, 0)
+
+
 def kernel_terms(u, back, kg):
     rows, width, ch = u.shape[1] - 2, u.shape[2], u.shape[3]
     kg[...] = jnp.zeros_like(kg)
@@ -230,7 +287,7 @@
 def step_kernel(
     x, w1, w2, sl, sh, kl_in, kh_in, al_in, ah_in,
     mism_s, o_low, o_high,
-    xs, w1s, w2s, vs, ys, tgt, fh, gate, kl, kh, p_low, p_high,
+    xs, w1s, w2s, vs, tmp, tgt, fh, gate, kl, kh, p_low, p_high, pt_low, pt_high,
     ulb, uhb, ul, uh, s_low, s_high, r_low, r_high,
     b_low, b_high, kg_low, kg_high, fine, g_low, g_high,
     *rest,
@@ -322,10 +379,12 @@
     c_sh.wait()
     for c in c_k:
         c.wait()
+    pt_low[...] = p_low[...].astype(F32).T.astype(BF16)
+    pt_high[...] = p_high[...].astype(F32).T.astype(BF16)
     widen(ulb, ul, 1, 8)
-    widen(uhb, uh, 1, 16)
+    widen_fine(uhb, tmp, uh, 1, 16)
     depthwise(ul, kl, s_low, 1, 6)
-    depthwise(uh, kh, s_high, 1, 14)
+    depthwise_fine(uh, kh, s_high, 1, 14)
 
     for c in c_x + c_w1:
         c.wait()
@@ -349,31 +408,36 @@
         xs[9] = jnp.zeros((32, 1024), BF16)
 
     for f in range(2):
-        acc = None
-        for dh in range(3):
-            part = dot(
-                xs[dh : dh + 8].reshape(256, 1024), w1s[dh, (1 - f) * 512 : (1 - f) * 512 + 1024, :]
+        col = []
+        for j in range(3):
+            acc = None
+            for dh in range(3):
+                part = dot(
+                    xs[dh : dh + 8].reshape(256, 1024),
+                    w1s[dh, (1 - f) * 512 : (1 - f) * 512 + 1024, j * 256 : (j + 1) * 256],
+                )
+                acc = part if acc is None else acc + part
+            col.append(acc)
+        tgt[f] = (from_left(col[0], 32) + col[1] + from_right(col[2], 32)).astype(BF16)
+
+    @pl.when(me < last)
+    def _():
+        down[4].start()
+
+    @pl.when(me > 0)
+    def _():
+        up[4].start()
+
+    def gate_rows(v, lo, hi, f):
+        wide = v.astype(F32)
+        val = wide / (1.0 + jnp.exp(-wide))
+        for n, moved in enumerate((from_left(val, 32), val, from_right(val, 32))):
+            gate[n, lo:hi, :, f * 256 : (f + 1) * 256] = moved.astype(BF16).reshape(
+                hi - lo, 32, 256
             )
-            acc = part if acc is None else acc + part
-        ys[:, :768] = acc
-        tgt[f] = (
-            from_left(ys[:, 0:256], 32) + ys[:, 256:512] + from_right(ys[:, 512:768], 32)
-        ).astype(BF16)
-
-    @pl.when(me < last)
-    def _():
-        down[4].start()
-
-    @pl.when(me > 0)
-    def _():
-        up[4].start()
-
-    def gated(v):
-        wide = v.astype(F32)
-        return (wide / (1.0 + jnp.exp(-wide))).astype(BF16)
-
-    for f in range(2):
-        gate[1:9, :, f * 256 : (f + 1) * 256] = gated(tgt[f]).reshape(8, 32, 256)
+
+    for f in range(2):
+        gate_rows(tgt[f], 1, 9, f)
 
     @pl.when(me > 0)
     def _():
@@ -400,20 +464,18 @@
     for first in (0, 9):
         widen(ulb, ul, first, 1)
     for first in (0, 17):
-        widen(uhb, uh, first, 1)
+        widen_fine(uhb, tmp, uh, first, 1)
     for first in (0, 7):
         depthwise(ul, kl, s_low, first, 1)
     for first in (0, 15):
-        depthwise(uh, kh, s_high, first, 1)
+        depthwise_fine(uh, kh, s_high, first, 1)
 
     for f in range(2):
         rows = slice(f * 256, (f + 1) * 256)
         res = dot(s_low[rows, :], p_low[...]) - tgt[f].astype(F32)
         resid = (res * scale_low).astype(BF16)
         r_low[rows, :] = resid
-        b_low[rows, :] = lax.dot_general(
-            resid, p_low[...], (((1,), (1,)), ((), ())), preferred_element_type=F32
-        )
+    b_low[...] = dot(r_low[...], pt_low[...])
     a_low = lax.dot_general(
         s_low[...], r_low[...], (((0,), (0,)), ((), ())), preferred_element_type=F32
     )
@@ -430,41 +492,51 @@
     def _():
         down[4].wait_recv()
         for f in range(2):
-            gate[0, :, f * 256 : (f + 1) * 256] = gated(fh[0, f])
+            gate_rows(fh[0, f], 0, 1, f)
 
     @pl.when(me == 0)
     def _():
-        gate[0] = jnp.zeros((32, 512), BF16)
+        for n in range(3):
+            gate[n, 0] = jnp.zeros((32, 512), BF16)
 
     @pl.when(me < last)
     def _():
         up[4].wait_recv()
         for f in range(2):
-            gate[9, :, f * 256 : (f + 1) * 256] = gated(fh[1, f])
+            gate_rows(fh[1, f], 9, 10, f)
 
     @pl.when(me == last)
     def _():
-        gate[9] = jnp.zeros((32, 512), BF16)
+        for n in range(3):
+            gate[n, 9] = jnp.zeros((32, 512), BF16)
 
     for f in range(2):
         for pr in range(2):
-            acc = None
-            for a in range(2):
-                part = dot(
-                    gate[pr + a : pr + a + 8].reshape(256, 512),
-                    vs[pr * 2 + a, (1 - f) * 256 : (1 - f) * 256 + 512, :],
-                )
-                acc = part if acc is None else acc + part
-            ys[...] = acc
-            even = from_left(ys[:, 0:256], 32) + ys[:, 256:512]
-            odd = ys[:, 512:768] + from_right(ys[:, 768:1024], 32)
-            for pc, val in enumerate((even, odd)):
+            for pc in range(2):
+                at = (f * 4 + pr * 2 + pc) * 256
+                rows = slice(at, at + 256)
+                res = dot(s_high[rows, :], p_high[...])
+                for a in range(2):
+                    for b in range(2):
+                        j = pc * 2 + b
+                        res += dot(
+                            gate[pc + b, pr + a : pr + a + 8].reshape(256, 512),
+                            vs[
+                                pr * 2 + a,
+                                (1 - f) * 256 : (1 - f) * 256 + 512,
+                                j * 256 : (j + 1) * 256,
+                            ],
+                        )
+                resid = (res * scale_high).astype(BF16)
+                r_high[rows, :] = resid
                 for r in range(8):
-                    at = (f * 16 + 2 * r + pr) * 64 + pc
+                    to = (f * 16 + 2 * r + pr) * 64 + pc
                     for half in range(2):
-                        fine[half, pl.ds(at, 32, stride=2), :] = val[
+                        fine[half, pl.ds(to, 32, stride=2), :] = res[
                             r * 32 : (r + 1) * 32, half * 128 : (half + 1) * 128
                         ]
+        half = slice(f * 1024, (f + 1) * 1024)
+        b_high[half, :] = dot(r_high[half, :], pt_high[...])
         if f == 0:
             red_low.core_end()
             red_low.y_start()
@@ -472,26 +544,22 @@
             red_low.y_end()
             red_low.z_start()
 
-    def fine_body(q, _):
-        rows = pl.ds(pl.multiple_of(q * 256, 256), 256)
-        target = jnp.concatenate([fine[0, rows, :], fine[1, rows, :]], axis=1)
-        target = target.astype(BF16).astype(F32)
-        res = dot(s_high[rows, :], p_high[...]) - target
-        mism_s[rows, :] = res.astype(BF16)
-        resid = (res * scale_high).astype(BF16)
-        r_high[rows, :] = resid
-        b_high[rows, :] = lax.dot_general(
-            resid, p_high[...], (((1,), (1,)), ((), ())), preferred_element_type=F32
-        )
-        return 0
-
-    lax.fori_loop(0, 8, fine_body, 0)
+    def emit(first, count):
+        def body(q, _):
+            rows = pl.ds(pl.multiple_of(q * 128, 128), 128)
+            mism_s[rows, :] = jnp.concatenate(
+                [fine[0, rows, :], fine[1, rows, :]], axis=1
+            ).astype(BF16)
+            return 0
+
+        lax.fori_loop(first, first + count, body, 0)
+
     red_low.z_end()
     red_low.x_start()
     a_high = lax.dot_general(
         s_high[...], r_high[...], (((0,), (0,)), ((), ())), preferred_element_type=F32
     )
-    kernel_terms(uh, b_high, kg_high)
+    kernel_terms_fine(uh, b_high, kg_high)
     k_high = kernel_rows(kg_high)
     for b in range(16):
         i = (b % 8) * 2 + b // 8
@@ -504,8 +572,10 @@
     o_low[...] = red_low.x_end()
     red_high.core_end()
     red_high.y_start()
+    emit(0, 6)
     red_high.y_end()
     red_high.z_start()
+    emit(6, 10)
     red_high.z_end()
     red_high.x_start()
     o_high[...] = red_high.x_end()
@@ -552,18 +622,20 @@
             v((3, 1536, 768), BF16),
             v((3, 3, 3, 256, 256), BF16),
             v((4, 768, 1024), BF16),
-            v((256, 1024), F32),
+            v((64, 128), F32),
             v((2, 256, 256), BF16),
             v((2, 2, 32, 256), BF16),
-            v((10, 32, 512), BF16),
+            v((3, 10, 32, 512), BF16),
             v((3, 3, 3, 256), F32),
             v((3, 3, 3, 128), F32),
             v((256, 256), BF16),
             v((128, 256), BF16),
+            v((256, 256), BF16),
+            v((256, 128), BF16),
             v((2, 10, 32, 256), BF16),
             v((2, 18, 64, 128), BF16),
             v((2, 10, 32, 256), F32),
-            v((2, 18, 64, 128), F32),
+            v((2, 2, 18, 32, 128), F32),
             v((512, 256), BF16),
             v((2048, 128), BF16),
             v((512, 256), BF16),

time: 50.7 us -> 49.6 us (0.978)
  Pallas kernels: 49.9 us -> 48.9 us
    pallas_call x1, Pallas kernels: 48.3 us -> 47.3 us  [step_call(): pl.pallas_call(step_kernel, out_shape=(jax.ShapeDtypeStruct((2048, 256),...]
where the time goes in v4:
time: 49.6 us; the launch traced here: 49.5 us
  Pallas kernels  48.9 us (99%)
  between operations  0.64 us (1%)
    pallas_call x1, Pallas kernels, step_call(): pl.pallas_call(step_kernel, out_shape=(jax.ShapeDtypeStruct((2048, 256),...  47.3 us
    pallas_call x1, Pallas kernels, on_device(): pl.pallas_call(unpack_kernel, out_shape=(jax.ShapeDtypeStruct((1, 2, 16,...  1.61 us

profile of v4, /device:TPU:2, one launch (start us, length us, event | category | flops | bytes accessed | tf_op | source)
XLA Modules:
  0.0 49.5 jit_solution(16398760102375298206)
XLA Ops:
  0.6 47.3 %step.1 = (bf16[2048,256]{1,0:T(8,128)(2,1)S(1)}, f32[16,384]{1,0:T(8,128)S(1)}, f32[16,256]{1,0:T(8,128)S(1)}) custom-call(bf16[1,2,8,32,512]{4,3,2,1,0:T(8,128)(2,1)} %x.1, bf16[3,3,3,512,256]{4,3,2,1,0:T(8,128)(2,1)} %w1.1, bf16[3,3,3,256,256]{4,3,2,1,0:T(8,128)(2,1)} %w2.1, bf16[1,2,8,32,256]{4,3,2,1,0:T(8,128)(2,1)} %sl.1, ...), custom_call_target="tpu_custom_call" | custom-call | tf_op jit(solution)/shard_map/step/pallas_call | solution.py:611
  47.9 1.6 %unpack.1 = (bf16[1,2,16,64,256]{4,3,2,1,0:T(8,128)(2,1)}, f32[16,256]{1,0:T(8,128)}, f32[3,3,3,16]{3,2,1,0:T(4,128)}, f32[8,256]{1,0:T(8,128)}, f32[3,3,3,8]{3,2,1,0:T(4,128)}) custom-call(bf16[2048,256]{1,0:T(8,128)(2,1)S(1)} %get-tuple-element.13.mism_s, f32[16,384]{1,0:T(8,128)S(1)} %get-tuple-element.14.low, f32[16,256]{1,0:T(8,128)S(1)} %get-tuple-element.15.high), custom_call_target="tpu_custom_call" | custom-call | tf_op jit(solution)/shard_map/unpack/pallas_call | solution.py:690

commit v5 on v4

--- a/solution.py
+++ b/solution.py
@@ -122,9 +122,8 @@
         lax.fori_loop(0, count, body, 0)
 
 
-def kernel_terms_fine(u, back, kg):
-    kg[...] = jnp.zeros_like(kg)
-    for f in range(2):
+def kernel_terms_fine(u, back, kg, frames):
+    for f in frames:
 
         def body(r, _):
             be, bo = back[fine_rows(f, r, 0), :], back[fine_rows(f, r, 1), :]
@@ -188,8 +187,10 @@
         return ((y * 2 + zh) * 2 + core, zl * 4 + x)
 
     def partners(self):
-        out = [self.dev(core=1 - self.core)]
-        out += [self.dev(y=lax.rem(self.y + d, 4)) for d in range(1, 4)]
+        out = []
+        for d in range(1, 8):
+            to = lax.rem(self.core * 4 + self.y + d, 8)
+            out.append(self.dev(core=to // 4, y=lax.rem(to, 4)))
         out += [self.dev(z=lax.rem(self.z + d, 8)) for d in range(1, 8)]
         out += [self.dev(x=lax.rem(self.x + d, 4)) for d in range(1, 4)]
         return out
@@ -236,10 +237,31 @@
         for c in self.live:
             c.wait()
         r2 = self.r2
-        self.h2[...] = (
+        self.h2[:, 0 : r2.shape[2]] = (
             self.h1[pl.ds(pl.multiple_of(t.y * 32, 32), 32), :]
             + (r2[0].astype(F32) + r2[1].astype(F32) + r2[2].astype(F32))
         ).astype(BF16)
+
+    def direct_start(self, g, sk, rk):
+        t = self.here
+        sk[...] = g[...].astype(BF16)
+        self.direct = []
+        for d in range(1, 8):
+            to = lax.rem(t.core * 4 + t.y + d, 8)
+            rows = pl.ds(pl.multiple_of(to * 32, 32), 32)
+            peer = t.dev(core=to // 4, y=lax.rem(to, 4))
+            self.direct.append(self.copy(sk.at[rows, :], rk.at[d - 1], 13 + d, peer))
+        for c in self.direct:
+            c.start()
+
+    def direct_end(self, g, rk):
+        t = self.here
+        for c in self.direct:
+            c.wait()
+        total = g[pl.ds(pl.multiple_of((t.core * 4 + t.y) * 32, 32), 32), :]
+        for d in range(7):
+            total += rk[d].astype(F32)
+        self.h2[:, 128:256] = total.astype(BF16)
 
     def share_start(self, source, slots, mine, size, base, peer):
         cs = []
@@ -249,10 +271,10 @@
         for c in cs:
             c.start()
         slots[mine] = source(mine)[...]
-        self.live = cs
+        self.shared = cs
 
     def share_end(self, source, slots, mine, size, base, peer):
-        for c in self.live:
+        for c in self.shared:
             c.wait_send()
         for d in range(1, size):
             came = lax.rem(mine + size - d, size)
@@ -290,7 +312,7 @@
     xs, w1s, w2s, vs, tmp, tgt, fh, gate, kl, kh, p_low, p_high, pt_low, pt_high,
     ulb, uhb, ul, uh, s_low, s_high, r_low, r_high,
     b_low, b_high, kg_low, kg_high, fine, g_low, g_high,
-    *rest,
+    g_kern, s_kern, r_kern, *rest,
 ):
     bufs_low, bufs_high = rest[:9], rest[9:18]
     sem, halo_snd, halo_rcv, snd_low, rcv_low, snd_high, rcv_high = rest[18:]
@@ -330,9 +352,6 @@
         for dt in range(3)
         for dw in range(3)
     ]
-
-    c_w2.wait()
-    build_taps(w2s, vs)
 
     inner = jnp.logical_and(me > 0, me < last)
 
@@ -374,6 +393,9 @@
     def _():
         for c in up[:4]:
             c.start()
+
+    c_w2.wait()
+    build_taps(w2s, vs)
 
     c_sl.wait()
     c_sh.wait()
@@ -554,30 +576,36 @@
 
         lax.fori_loop(first, first + count, body, 0)
 
-    red_low.z_end()
-    red_low.x_start()
     a_high = lax.dot_general(
         s_high[...], r_high[...], (((0,), (0,)), ((), ())), preferred_element_type=F32
     )
-    kernel_terms_fine(uh, b_high, kg_high)
+    for b in range(16):
+        i = (b % 8) * 2 + b // 8
+        g_high[b * 16 : b * 16 + 8, :] = a_high[i * 8 : (i + 1) * 8, 0:128]
+        g_high[b * 16 + 8 : b * 16 + 16, :] = a_high[i * 8 : (i + 1) * 8, 128:256]
+    red_high = Reduction(here, g_high, bufs_high, snd_high, rcv_high)
+    red_high.core_start()
+    kg_high[...] = jnp.zeros_like(kg_high)
+    kernel_terms_fine(uh, b_high, kg_high, (0,))
+    red_high.core_end()
+    red_high.y_start()
+    kernel_terms_fine(uh, b_high, kg_high, (1,))
     k_high = kernel_rows(kg_high)
     for b in range(16):
         i = (b % 8) * 2 + b // 8
-        g_high[b * 16 : b * 16 + 8, 0:128] = a_high[i * 8 : (i + 1) * 8, 0:128]
-        g_high[b * 16 + 8 : b * 16 + 16, 0:128] = a_high[i * 8 : (i + 1) * 8, 128:256]
-        g_high[b * 16 : b * 16 + 8, 128:256] = k_high[i * 8 : (i + 1) * 8]
-        g_high[b * 16 + 8 : b * 16 + 16, 128:256] = jnp.zeros((8, 128), F32)
-    red_high = Reduction(here, g_high, bufs_high, snd_high, rcv_high)
-    red_high.core_start()
-    o_low[...] = red_low.x_end()
-    red_high.core_end()
-    red_high.y_start()
-    emit(0, 6)
+        g_kern[b * 16 : b * 16 + 8, :] = k_high[i * 8 : (i + 1) * 8]
+        g_kern[b * 16 + 8 : b * 16 + 16, :] = jnp.zeros((8, 128), F32)
+    red_high.direct_start(g_kern, s_kern, r_kern)
     red_high.y_end()
+    emit(0, 8)
+    red_high.direct_end(g_kern, r_kern)
     red_high.z_start()
-    emit(6, 10)
+    red_low.z_end()
+    red_low.x_start()
+    emit(8, 8)
     red_high.z_end()
     red_high.x_start()
+    o_low[...] = red_low.x_end()
     o_high[...] = red_high.x_end()
 
     @pl.when(me < last)
@@ -595,17 +623,17 @@
     v = pltpu.VMEM
     dma = pltpu.SemaphoreType.DMA
 
-    def reduction_buffers(lanes):
+    def reduction_buffers(lanes, later):
         return [
             v((128, lanes), BF16),
             v((128, lanes), BF16),
             v((128, lanes), F32),
             v((128, lanes), BF16),
             v((3, 32, lanes), BF16),
-            v((32, lanes), BF16),
-            v((8, 16, lanes), BF16),
-            v((16, lanes), BF16),
-            v((4, 16, lanes), BF16),
+            v((32, later), BF16),
+            v((8, 16, later), BF16),
+            v((16, later), BF16),
+            v((4, 16, later), BF16),
         ]
 
     return pl.pallas_call(
@@ -646,16 +674,19 @@
             v((27, 8, 128), F32),
             v((2, 2048, 128), F32),
             v((256, 384), F32),
-            v((256, 256), F32),
-            *reduction_buffers(384),
-            *reduction_buffers(256),
+            v((256, 128), F32),
+            v((256, 128), F32),
+            v((256, 128), BF16),
+            v((7, 32, 128), BF16),
+            *reduction_buffers(384, 384),
+            *reduction_buffers(128, 256),
             dma((18,)),
             dma((2, 5)),
             dma((2, 5)),
             dma((14,)),
             dma((14,)),
-            dma((14,)),
-            dma((14,)),
+            dma((21,)),
+            dma((21,)),
         ],
         compiler_params=pltpu.CompilerParams(
             collective_id=0, has_side_effects=True, vmem_limit_bytes=STEP_VMEM

time: 49.6 us -> 43.3 us (0.87)
  Pallas kernels: 48.9 us -> 42.5 us
    pallas_call x1, Pallas kernels: 47.3 us -> 40.9 us  [step_call(): pl.pallas_call(step_kernel, out_shape=(jax.ShapeDtypeStruct((2048, 256),...]
where the time goes in v5:
time: 43.3 us; the launch traced here: 43.2 us
  Pallas kernels  42.5 us (98%)
  between operations  0.64 us (1%)
    pallas_call x1, Pallas kernels, step_call(): pl.pallas_call(step_kernel, out_shape=(jax.ShapeDtypeStruct((2048, 256),...  40.9 us
    pallas_call x1, Pallas kernels, on_device(): pl.pallas_call(unpack_kernel, out_shape=(jax.ShapeDtypeStruct((1, 2, 16,...  1.61 us

profile of v5, /device:TPU:2, one launch (start us, length us, event | category | flops | bytes accessed | tf_op | source)
XLA Modules:
  0.0 43.2 jit_solution(8143771962349643426)
XLA Ops:
  0.6 40.9 %step.1 = (bf16[2048,256]{1,0:T(8,128)(2,1)S(1)}, f32[16,384]{1,0:T(8,128)S(1)}, f32[16,256]{1,0:T(8,128)S(1)}) custom-call(bf16[1,2,8,32,512]{4,3,2,1,0:T(8,128)(2,1)} %x.1, bf16[3,3,3,512,256]{4,3,2,1,0:T(8,128)(2,1)} %w1.1, bf16[3,3,3,256,256]{4,3,2,1,0:T(8,128)(2,1)} %w2.1, bf16[1,2,8,32,256]{4,3,2,1,0:T(8,128)(2,1)} %sl.1, ...), custom_call_target="tpu_custom_call" | custom-call | tf_op jit(solution)/shard_map/step/pallas_call | solution.py:639
  41.6 1.6 %unpack.1 = (bf16[1,2,16,64,256]{4,3,2,1,0:T(8,128)(2,1)}, f32[16,256]{1,0:T(8,128)}, f32[3,3,3,16]{3,2,1,0:T(4,128)}, f32[8,256]{1,0:T(8,128)}, f32[3,3,3,8]{3,2,1,0:T(4,128)}) custom-call(bf16[2048,256]{1,0:T(8,128)(2,1)S(1)} %get-tuple-element.13.mism_s, f32[16,384]{1,0:T(8,128)S(1)} %get-tuple-element.14.low, f32[16,256]{1,0:T(8,128)S(1)} %get-tuple-element.15.high), custom_call_target="tpu_custom_call" | custom-call | tf_op jit(solution)/shard_map/unpack/pallas_call | solution.py:721

commit v6 on v5

--- a/solution.py
+++ b/solution.py
@@ -98,6 +98,8 @@
 
 
 def fine_rows(f, r, pc):
+    if isinstance(r, int):
+        return pl.ds((f * 4 + r % 2 * 2 + pc) * 256 + r // 2 * 32, 32)
     return pl.ds(pl.multiple_of((f * 4 + lax.rem(r, 2) * 2 + pc) * 256 + r // 2 * 32, 32), 32)
 
 
@@ -122,22 +124,24 @@
         lax.fori_loop(0, count, body, 0)
 
 
-def kernel_terms_fine(u, back, kg, frames):
-    for f in frames:
-
-        def body(r, _):
-            be, bo = back[fine_rows(f, r, 0), :], back[fine_rows(f, r, 1), :]
-            be_right, bo_left = from_right(be, 32), from_left(bo, 32)
-            for g in range(2):
-                for dh in range(3):
-                    e, o = u[0, g, r + dh], u[1, g, r + dh]
-                    terms = (be_right * o + bo * e, be * e + bo * o, be * o + bo_left * e)
-                    for dw in range(3):
-                        tap = (g - f + 1) * 9 + dh * 3 + dw
-                        kg[tap] += jnp.sum(terms[dw].reshape(4, 8, 128), axis=0)
-            return 0
-
-        lax.fori_loop(0, 16, body, 0)
+def kernel_term_row_fine(u, back, kg, f, r):
+    be, bo = back[fine_rows(f, r, 0), :], back[fine_rows(f, r, 1), :]
+    be_right, bo_left = from_right(be, 32), from_left(bo, 32)
+    for g in range(2):
+        for dh in range(3):
+            e, o = u[0, g, r + dh], u[1, g, r + dh]
+            terms = (be_right * o + bo * e, be * e + bo * o, be * o + bo_left * e)
+            for dw in range(3):
+                tap = (g - f + 1) * 9 + dh * 3 + dw
+                kg[tap] += jnp.sum(terms[dw].reshape(4, 8, 128), axis=0)
+
+
+def kernel_terms_fine(u, back, kg, f, first, count):
+    def body(step, _):
+        kernel_term_row_fine(u, back, kg, f, first + step)
+        return 0
+
+    lax.fori_loop(0, count, body, 0)
 
 
 def kernel_terms(u, back, kg):
@@ -248,7 +252,7 @@
         self.direct = []
         for d in range(1, 8):
             to = lax.rem(t.core * 4 + t.y + d, 8)
-            rows = pl.ds(pl.multiple_of(to * 32, 32), 32)
+            rows = pl.ds(pl.multiple_of(to * 16, 16), 16)
             peer = t.dev(core=to // 4, y=lax.rem(to, 4))
             self.direct.append(self.copy(sk.at[rows, :], rk.at[d - 1], 13 + d, peer))
         for c in self.direct:
@@ -258,10 +262,11 @@
         t = self.here
         for c in self.direct:
             c.wait()
-        total = g[pl.ds(pl.multiple_of((t.core * 4 + t.y) * 32, 32), 32), :]
+        total = g[pl.ds(pl.multiple_of((t.core * 4 + t.y) * 16, 16), 16), :]
         for d in range(7):
             total += rk[d].astype(F32)
-        self.h2[:, 128:256] = total.astype(BF16)
+        self.h2[0:8, 128:256] = total[0:8].astype(BF16)
+        self.h2[16:24, 128:256] = total[8:16].astype(BF16)
 
     def share_start(self, source, slots, mine, size, base, peer):
         cs = []
@@ -509,6 +514,8 @@
         g_low[b * 16 : (b + 1) * 16, 256:384] = k_low[i * 16 : (i + 1) * 16]
     red_low = Reduction(here, g_low, bufs_low, snd_low, rcv_low)
     red_low.core_start()
+    kg_high[...] = jnp.zeros_like(kg_high)
+    bufs_high[5][...] = jnp.zeros((32, 256), BF16)
 
     @pl.when(me > 0)
     def _():
@@ -551,6 +558,9 @@
                         )
                 resid = (res * scale_high).astype(BF16)
                 r_high[rows, :] = resid
+                if f == 1:
+                    for n in range(4):
+                        kernel_term_row_fine(uh, b_high, kg_high, 0, (pr * 2 + pc) * 4 + n)
                 for r in range(8):
                     to = (f * 16 + 2 * r + pr) * 64 + pc
                     for half in range(2):
@@ -562,9 +572,6 @@
         if f == 0:
             red_low.core_end()
             red_low.y_start()
-        else:
-            red_low.y_end()
-            red_low.z_start()
 
     def emit(first, count):
         def body(q, _):
@@ -585,16 +592,16 @@
         g_high[b * 16 + 8 : b * 16 + 16, :] = a_high[i * 8 : (i + 1) * 8, 128:256]
     red_high = Reduction(here, g_high, bufs_high, snd_high, rcv_high)
     red_high.core_start()
-    kg_high[...] = jnp.zeros_like(kg_high)
-    kernel_terms_fine(uh, b_high, kg_high, (0,))
+    kernel_terms_fine(uh, b_high, kg_high, 1, 0, 12)
     red_high.core_end()
     red_high.y_start()
-    kernel_terms_fine(uh, b_high, kg_high, (1,))
+    red_low.y_end()
+    red_low.z_start()
+    kernel_terms_fine(uh, b_high, kg_high, 1, 12, 4)
     k_high = kernel_rows(kg_high)
     for b in range(16):
         i = (b % 8) * 2 + b // 8
-        g_kern[b * 16 : b * 16 + 8, :] = k_high[i * 8 : (i + 1) * 8]
-        g_kern[b * 16 + 8 : b * 16 + 16, :] = jnp.zeros((8, 128), F32)
+        g_kern[b * 8 : (b + 1) * 8, :] = k_high[i * 8 : (i + 1) * 8]
     red_high.direct_start(g_kern, s_kern, r_kern)
     red_high.y_end()
     emit(0, 8)
@@ -675,9 +682,9 @@
             v((2, 2048, 128), F32),
             v((256, 384), F32),
             v((256, 128), F32),
-            v((256, 128), F32),
-            v((256, 128), BF16),
-            v((7, 32, 128), BF16),
+            v((128, 128), F32),
+            v((128, 128), BF16),
+            v((7, 16, 128), BF16),
             *reduction_buffers(384, 384),
             *reduction_buffers(128, 256),
             dma((18,)),
@@ -698,9 +705,12 @@
 def unpack_kernel(mism_s, low, high, mism, o_al, o_kl, o_ah, o_kh, sem):
     cs = [
         pltpu.make_async_copy(
-            mism_s.reshape(2, 16, 64, 256).at[f], mism.at[0, f], sem.at[f]
+            mism_s.reshape(2, 16, 64, 256).at[f, q * 4 : q * 4 + 4],
+            mism.at[0, f, q * 4 : q * 4 + 4],
+            sem.at[f * 4 + q],
         )
         for f in range(2)
+        for q in range(4)
     ]
     for c in cs:
         c.start()
@@ -729,7 +739,7 @@
         ),
         in_specs=[VM] * 3,
         out_specs=(HBM, VM, VM, VM, VM),
-        scratch_shapes=[pltpu.SemaphoreType.DMA((2,))],
+        scratch_shapes=[pltpu.SemaphoreType.DMA((8,))],
         compiler_params=pltpu.CompilerParams(vmem_limit_bytes=4 << 20),
         name="unpack",
     )(*step_call(*args))

time: 43.3 us -> 41.1 us (0.949)
  Pallas kernels: 42.5 us -> 40.4 us
    pallas_call x1, Pallas kernels: 40.9 us -> 38.8 us  [step_call(): pl.pallas_call(step_kernel, out_shape=(jax.ShapeDtypeStruct((2048, 256),...]
where the time goes in v6:
time: 41.1 us; the launch traced here: 41 us
  Pallas kernels  40.4 us (98%)
  between operations  0.64 us (2%)
    pallas_call x1, Pallas kernels, step_call(): pl.pallas_call(step_kernel, out_shape=(jax.ShapeDtypeStruct((2048, 256),...  38.8 us
    pallas_call x1, Pallas kernels, on_device(): pl.pallas_call(unpack_kernel, out_shape=(jax.ShapeDtypeStruct((1, 2, 16,...  1.65 us

profile of v6, /device:TPU:2, one launch (start us, length us, event | category | flops | bytes accessed | tf_op | source)
XLA Modules:
  0.0 41.0 jit_solution(10073744202377562274)
XLA Ops:
  0.6 38.8 %step.1 = (bf16[2048,256]{1,0:T(8,128)(2,1)S(1)}, f32[16,384]{1,0:T(8,128)S(1)}, f32[16,256]{1,0:T(8,128)S(1)}) custom-call(bf16[1,2,8,32,512]{4,3,2,1,0:T(8,128)(2,1)} %x.1, bf16[3,3,3,512,256]{4,3,2,1,0:T(8,128)(2,1)} %w1.1, bf16[3,3,3,256,256]{4,3,2,1,0:T(8,128)(2,1)} %w2.1, bf16[1,2,8,32,256]{4,3,2,1,0:T(8,128)(2,1)} %sl.1, ...), custom_call_target="tpu_custom_call" | custom-call | tf_op jit(solution)/shard_map/step/pallas_call | solution.py:646
  39.4 1.6 %unpack.1 = (bf16[1,2,16,64,256]{4,3,2,1,0:T(8,128)(2,1)}, f32[16,256]{1,0:T(8,128)}, f32[3,3,3,16]{3,2,1,0:T(4,128)}, f32[8,256]{1,0:T(8,128)}, f32[3,3,3,8]{3,2,1,0:T(4,128)}) custom-call(bf16[2048,256]{1,0:T(8,128)(2,1)S(1)} %get-tuple-element.13.mism_s, f32[16,384]{1,0:T(8,128)S(1)} %get-tuple-element.14.low, f32[16,256]{1,0:T(8,128)S(1)} %get-tuple-element.15.high), custom_call_target="tpu_custom_call" | custom-call | tf_op jit(solution)/shard_map/unpack/pallas_call | solution.py:731

commit v7 on v6

--- a/solution.py
+++ b/solution.py
@@ -314,7 +314,7 @@
 def step_kernel(
     x, w1, w2, sl, sh, kl_in, kh_in, al_in, ah_in,
     mism_s, o_low, o_high,
-    xs, w1s, w2s, vs, tmp, tgt, fh, gate, kl, kh, p_low, p_high, pt_low, pt_high,
+    xs, w1s, w2s, vs, tmp, mid, tgt, fh, gate, kl, kh, p_low, p_high, pt_low, pt_high,
     ulb, uhb, ul, uh, s_low, s_high, r_low, r_high,
     b_low, b_high, kg_low, kg_high, fine, g_low, g_high,
     g_kern, s_kern, r_kern, *rest,
@@ -416,6 +416,16 @@
     for c in c_x + c_w1:
         c.wait()
 
+    def conv_part(f, j, dh):
+        return dot(
+            xs[dh : dh + 8].reshape(256, 1024),
+            w1s[dh, (1 - f) * 512 : (1 - f) * 512 + 1024, j * 256 : (j + 1) * 256],
+        )
+
+    for f in range(2):
+        for j in range(3):
+            mid[f, j] = conv_part(f, j, 1)
+
     @pl.when(me > 0)
     def _():
         for c in down[:2]:
@@ -435,16 +445,7 @@
         xs[9] = jnp.zeros((32, 1024), BF16)
 
     for f in range(2):
-        col = []
-        for j in range(3):
-            acc = None
-            for dh in range(3):
-                part = dot(
-                    xs[dh : dh + 8].reshape(256, 1024),
-                    w1s[dh, (1 - f) * 512 : (1 - f) * 512 + 1024, j * 256 : (j + 1) * 256],
-                )
-                acc = part if acc is None else acc + part
-            col.append(acc)
+        col = [mid[f, j] + conv_part(f, j, 0) + conv_part(f, j, 2) for j in range(3)]
         tgt[f] = (from_left(col[0], 32) + col[1] + from_right(col[2], 32)).astype(BF16)
 
     @pl.when(me < last)
@@ -595,14 +596,14 @@
     kernel_terms_fine(uh, b_high, kg_high, 1, 0, 12)
     red_high.core_end()
     red_high.y_start()
-    red_low.y_end()
-    red_low.z_start()
     kernel_terms_fine(uh, b_high, kg_high, 1, 12, 4)
     k_high = kernel_rows(kg_high)
     for b in range(16):
         i = (b % 8) * 2 + b // 8
         g_kern[b * 8 : (b + 1) * 8, :] = k_high[i * 8 : (i + 1) * 8]
     red_high.direct_start(g_kern, s_kern, r_kern)
+    red_low.y_end()
+    red_low.z_start()
     red_high.y_end()
     emit(0, 8)
     red_high.direct_end(g_kern, r_kern)
@@ -658,6 +659,7 @@
             v((3, 3, 3, 256, 256), BF16),
             v((4, 768, 1024), BF16),
             v((64, 128), F32),
+            v((2, 3, 256, 256), F32),
             v((2, 256, 256), BF16),
             v((2, 2, 32, 256), BF16),
             v((3, 10, 32, 512), BF16),
@@ -702,7 +704,7 @@
     )(*(pltpu.with_memory_space_constraint(v, pltpu.HBM) for v in (x, w1, w2, sl, sh, kl, kh, p_low, p_high)))
 
 
-def unpack_kernel(mism_s, low, high, mism, o_al, o_kl, o_ah, o_kh, sem):
+def unpack_kernel(mism_s, low, high, mism, o_al, o_kl, o_ah, o_kh, s_al, s_kl, s_ah, s_kh, sem):
     cs = [
         pltpu.make_async_copy(
             mism_s.reshape(2, 16, 64, 256).at[f, q * 4 : q * 4 + 4],
@@ -714,32 +716,36 @@
     ]
     for c in cs:
         c.start()
-    o_al[...] = low[:, 0:256]
-    o_ah[...] = jnp.concatenate([high[0:8, 0:128], high[8:16, 0:128]], axis=1)
+    s_al[...] = low[:, 0:256]
+    s_ah[...] = jnp.concatenate([high[0:8, 0:128], high[8:16, 0:128]], axis=1)
     low_k = jnp.concatenate([low[:, 256:384], jnp.zeros((112, 128), F32)], axis=0).T
     high_k = jnp.concatenate([high[0:8, 128:256], jnp.zeros((120, 128), F32)], axis=0).T
     for dt in range(3):
         for dh in range(3):
             n = (dt * 3 + dh) * 3
-            o_kl[dt, dh] = low_k[n : n + 3, 0:16]
-            o_kh[dt, dh] = high_k[n : n + 3, 0:8]
+            s_kl[dt, dh] = low_k[n : n + 3, 0:16]
+            s_kh[dt, dh] = high_k[n : n + 3, 0:8]
+    for n, (a, b) in enumerate(((s_al, o_al), (s_kl, o_kl), (s_ah, o_ah), (s_kh, o_kh))):
+        cs.append(pltpu.make_async_copy(a, b, sem.at[8 + n]))
+        cs[-1].start()
     for c in cs:
         c.wait()
 
 
 def on_device(*args):
+    shapes = ((16, 256), (3, 3, 3, 16), (8, 256), (3, 3, 3, 8))
     mism, a_low, k_low, a_high, k_high = pl.pallas_call(
         unpack_kernel,
         out_shape=(
             jax.ShapeDtypeStruct((1, 2, 16, 64, 256), BF16),
-            jax.ShapeDtypeStruct((16, 256), F32),
-            jax.ShapeDtypeStruct((3, 3, 3, 16), F32),
-            jax.ShapeDtypeStruct((8, 256), F32),
-            jax.ShapeDtypeStruct((3, 3, 3, 8), F32),
+            *(jax.ShapeDtypeStruct(n, F32) for n in shapes),
         ),
         in_specs=[VM] * 3,
-        out_specs=(HBM, VM, VM, VM, VM),
-        scratch_shapes=[pltpu.SemaphoreType.DMA((8,))],
+        out_specs=(HBM,) * 5,
+        scratch_shapes=[
+            *(pltpu.VMEM(n, F32) for n in shapes),
+            pltpu.SemaphoreType.DMA((12,)),
+        ],
         compiler_params=pltpu.CompilerParams(vmem_limit_bytes=4 << 20),
         name="unpack",
     )(*step_call(*args))

time: 41.1 us -> 39.7 us (0.966)
  Pallas kernels: 40.4 us -> 39 us
    pallas_call x1, Pallas kernels: 38.8 us -> 37.9 us  [step_call(): pl.pallas_call(step_kernel, out_shape=(jax.ShapeDtypeStruct((2048, 256),...]
    pallas_call x1, Pallas kernels: 1.65 us -> 1.07 us  [on_device(): pl.pallas_call(unpack_kernel, out_shape=(jax.ShapeDtypeStruct((1, 2, 16,...]
where the time goes in v7:
time: 39.7 us; the launch traced here: 39.6 us
  Pallas kernels  39 us (98%)
  between operations  0.64 us (2%)
    pallas_call x1, Pallas kernels, step_call(): pl.pallas_call(step_kernel, out_shape=(jax.ShapeDtypeStruct((2048, 256),...  37.9 us
    pallas_call x1, Pallas kernels, on_device(): pl.pallas_call(unpack_kernel, out_shape=(jax.ShapeDtypeStruct((1, 2, 16,...  1.07 us

profile of v7, /device:TPU:2, one launch (start us, length us, event | category | flops | bytes accessed | tf_op | source)
XLA Modules:
  0.0 39.6 jit_solution(6074254593272128585)
XLA Ops:
  0.6 37.9 %step.1 = (bf16[2048,256]{1,0:T(8,128)(2,1)S(1)}, f32[16,384]{1,0:T(8,128)S(1)}, f32[16,256]{1,0:T(8,128)S(1)}) custom-call(bf16[1,2,8,32,512]{4,3,2,1,0:T(8,128)(2,1)} %x.1, bf16[3,3,3,512,256]{4,3,2,1,0:T(8,128)(2,1)} %w1.1, bf16[3,3,3,256,256]{4,3,2,1,0:T(8,128)(2,1)} %w2.1, bf16[1,2,8,32,256]{4,3,2,1,0:T(8,128)(2,1)} %sl.1, ...), custom_call_target="tpu_custom_call" | custom-call | tf_op jit(solution)/shard_map/step/pallas_call | solution.py:647
  38.6 1.1 %unpack.1 = (bf16[1,2,16,64,256]{4,3,2,1,0:T(8,128)(2,1)}, f32[16,256]{1,0:T(8,128)}, f32[3,3,3,16]{3,2,1,0:T(4,128)}, f32[8,256]{1,0:T(8,128)}, f32[3,3,3,8]{3,2,1,0:T(4,128)}) custom-call(bf16[2048,256]{1,0:T(8,128)(2,1)S(1)} %get-tuple-element.13.mism_s, f32[16,384]{1,0:T(8,128)S(1)} %get-tuple-element.14.low, f32[16,256]{1,0:T(8,128)S(1)} %get-tuple-element.15.high), custom_call_target="tpu_custom_call" | custom-call | tf_op jit(solution)/shard_map/unpack/pallas_call | solution.py:737

commit v8 on v7

--- a/solution.py
+++ b/solution.py
@@ -201,9 +201,9 @@
 
 
 class Reduction:
-    def __init__(self, here, g, bufs, snd, rcv):
-        self.here, self.g = here, g
-        self.s1, self.r1, self.h1, self.s2, self.r2, self.h2, self.r4, self.h4, self.r5 = bufs
+    def __init__(self, here, bufs, snd, rcv):
+        self.here = here
+        self.h2, self.r4, self.h4, self.r5 = bufs
         self.snd, self.rcv = snd, rcv
 
     def copy(self, src, dst, n, peer):
@@ -212,61 +212,29 @@
             device_id=peer, device_id_type=MESH,
         )
 
-    def core_start(self):
+    def direct_start(self, g, sent, slots, base):
         t = self.here
-        self.s1[...] = self.g[pl.ds(pl.multiple_of((1 - t.core) * 128, 128), 128), :].astype(BF16)
-        self.live = [self.copy(self.s1, self.r1, 0, t.dev(core=1 - t.core))]
-        self.live[0].start()
-
-    def core_end(self):
-        t = self.here
-        self.live[0].wait()
-        self.h1[...] = self.g[pl.ds(pl.multiple_of(t.core * 128, 128), 128), :] + self.r1[
-            ...
-        ].astype(F32)
-
-    def y_start(self):
-        t = self.here
-        self.s2[...] = self.h1[...].astype(BF16)
-        self.live = []
-        for d in range(1, 4):
-            to = lax.rem(t.y + d, 4)
-            rows = pl.ds(pl.multiple_of(to * 32, 32), 32)
-            self.live.append(self.copy(self.s2.at[rows, :], self.r2.at[d - 1], d, t.dev(y=to)))
-        for c in self.live:
-            c.start()
-
-    def y_end(self):
-        t = self.here
-        for c in self.live:
-            c.wait()
-        r2 = self.r2
-        self.h2[:, 0 : r2.shape[2]] = (
-            self.h1[pl.ds(pl.multiple_of(t.y * 32, 32), 32), :]
-            + (r2[0].astype(F32) + r2[1].astype(F32) + r2[2].astype(F32))
-        ).astype(BF16)
-
-    def direct_start(self, g, sk, rk):
-        t = self.here
-        sk[...] = g[...].astype(BF16)
-        self.direct = []
+        size = slots.shape[1]
+        sent[...] = g[...].astype(BF16)
+        cs = []
         for d in range(1, 8):
             to = lax.rem(t.core * 4 + t.y + d, 8)
-            rows = pl.ds(pl.multiple_of(to * 16, 16), 16)
+            rows = pl.ds(pl.multiple_of(to * size, size), size)
             peer = t.dev(core=to // 4, y=lax.rem(to, 4))
-            self.direct.append(self.copy(sk.at[rows, :], rk.at[d - 1], 13 + d, peer))
-        for c in self.direct:
+            cs.append(self.copy(sent.at[rows, :], slots.at[d - 1], base + d, peer))
+        for c in cs:
             c.start()
-
-    def direct_end(self, g, rk):
+        return cs
+
+    def direct_end(self, cs, g, slots):
         t = self.here
-        for c in self.direct:
+        size = slots.shape[1]
+        for c in cs:
             c.wait()
-        total = g[pl.ds(pl.multiple_of((t.core * 4 + t.y) * 16, 16), 16), :]
+        total = g[pl.ds(pl.multiple_of((t.core * 4 + t.y) * size, size), size), :]
         for d in range(7):
-            total += rk[d].astype(F32)
-        self.h2[0:8, 128:256] = total[0:8].astype(BF16)
-        self.h2[16:24, 128:256] = total[8:16].astype(BF16)
+            total += slots[d].astype(F32)
+        return total
 
     def share_start(self, source, slots, mine, size, base, peer):
         cs = []
@@ -317,10 +285,10 @@
     xs, w1s, w2s, vs, tmp, mid, tgt, fh, gate, kl, kh, p_low, p_high, pt_low, pt_high,
     ulb, uhb, ul, uh, s_low, s_high, r_low, r_high,
     b_low, b_high, kg_low, kg_high, fine, g_low, g_high,
-    g_kern, s_kern, r_kern, *rest,
+    g_kern, s_lowg, r_lowg, s_highg, r_highg, s_kern, r_kern, *rest,
 ):
-    bufs_low, bufs_high = rest[:9], rest[9:18]
-    sem, halo_snd, halo_rcv, snd_low, rcv_low, snd_high, rcv_high = rest[18:]
+    bufs_low, bufs_high = rest[:4], rest[4:8]
+    sem, halo_snd, halo_rcv, snd_low, rcv_low, snd_high, rcv_high = rest[8:]
     here = Where()
     me, last = here.space, here.last
     scale_low = 1.0 / (16 * 2 * 128 * 32)
@@ -348,16 +316,6 @@
         return c
 
     c_w2 = load(w2, w2s)
-    c_sl = load(sl.at[0], ulb.at[:, 1:9])
-    c_sh = load(sh.at[0], uhb.at[:, 1:17])
-    c_k = [load(kl_in, kl), load(kh_in, kh), load(al_in, p_low), load(ah_in, p_high)]
-    c_x = [load(x.at[0, f], xs.at[1:9, :, f * 512 : (f + 1) * 512]) for f in range(2)]
-    c_w1 = [
-        load(w1.at[dt, :, dw], w1s.at[:, dt * 512 : (dt + 1) * 512, dw * 256 : (dw + 1) * 256])
-        for dt in range(3)
-        for dw in range(3)
-    ]
-
     inner = jnp.logical_and(me > 0, me < last)
 
     @pl.when(inner)
@@ -399,6 +357,16 @@
         for c in up[:4]:
             c.start()
 
+    c_sl = load(sl.at[0], ulb.at[:, 1:9])
+    c_sh = load(sh.at[0], uhb.at[:, 1:17])
+    c_k = [load(kl_in, kl), load(kh_in, kh), load(al_in, p_low), load(ah_in, p_high)]
+    c_x = [load(x.at[0, f], xs.at[1:9, :, f * 512 : (f + 1) * 512]) for f in range(2)]
+    c_w1 = [
+        load(w1.at[dt, :, dw], w1s.at[:, dt * 512 : (dt + 1) * 512, dw * 256 : (dw + 1) * 256])
+        for dt in range(3)
+        for dw in range(3)
+    ]
+
     c_w2.wait()
     build_taps(w2s, vs)
 
@@ -513,10 +481,10 @@
         i = (b % 8) * 2 + b // 8
         g_low[b * 16 : (b + 1) * 16, 0:256] = a_low[i * 16 : (i + 1) * 16]
         g_low[b * 16 : (b + 1) * 16, 256:384] = k_low[i * 16 : (i + 1) * 16]
-    red_low = Reduction(here, g_low, bufs_low, snd_low, rcv_low)
-    red_low.core_start()
+    red_low = Reduction(here, bufs_low, snd_low, rcv_low)
+    low_direct = red_low.direct_start(g_low, s_lowg, r_lowg, 13)
     kg_high[...] = jnp.zeros_like(kg_high)
-    bufs_high[5][...] = jnp.zeros((32, 256), BF16)
+    bufs_high[0][...] = jnp.zeros((32, 256), BF16)
 
     @pl.when(me > 0)
     def _():
@@ -570,10 +538,6 @@
                         ]
         half = slice(f * 1024, (f + 1) * 1024)
         b_high[half, :] = dot(r_high[half, :], pt_high[...])
-        if f == 0:
-            red_low.core_end()
-            red_low.y_start()
-
     def emit(first, count):
         def body(q, _):
             rows = pl.ds(pl.multiple_of(q * 128, 128), 128)
@@ -591,22 +555,21 @@
         i = (b % 8) * 2 + b // 8
         g_high[b * 16 : b * 16 + 8, :] = a_high[i * 8 : (i + 1) * 8, 0:128]
         g_high[b * 16 + 8 : b * 16 + 16, :] = a_high[i * 8 : (i + 1) * 8, 128:256]
-    red_high = Reduction(here, g_high, bufs_high, snd_high, rcv_high)
-    red_high.core_start()
-    kernel_terms_fine(uh, b_high, kg_high, 1, 0, 12)
-    red_high.core_end()
-    red_high.y_start()
-    kernel_terms_fine(uh, b_high, kg_high, 1, 12, 4)
+    red_high = Reduction(here, bufs_high, snd_high, rcv_high)
+    high_direct = red_high.direct_start(g_high, s_highg, r_highg, 13)
+    kernel_terms_fine(uh, b_high, kg_high, 1, 0, 16)
     k_high = kernel_rows(kg_high)
     for b in range(16):
         i = (b % 8) * 2 + b // 8
         g_kern[b * 8 : (b + 1) * 8, :] = k_high[i * 8 : (i + 1) * 8]
-    red_high.direct_start(g_kern, s_kern, r_kern)
-    red_low.y_end()
+    kern_direct = red_high.direct_start(g_kern, s_kern, r_kern, 20)
+    red_low.h2[...] = red_low.direct_end(low_direct, g_low, r_lowg).astype(BF16)
     red_low.z_start()
-    red_high.y_end()
     emit(0, 8)
-    red_high.direct_end(g_kern, r_kern)
+    red_high.h2[:, 0:128] = red_high.direct_end(high_direct, g_high, r_highg).astype(BF16)
+    total = red_high.direct_end(kern_direct, g_kern, r_kern).astype(BF16)
+    red_high.h2[0:8, 128:256] = total[0:8]
+    red_high.h2[16:24, 128:256] = total[8:16]
     red_high.z_start()
     red_low.z_end()
     red_low.x_start()
@@ -631,17 +594,12 @@
     v = pltpu.VMEM
     dma = pltpu.SemaphoreType.DMA
 
-    def reduction_buffers(lanes, later):
+    def reduction_buffers(lanes):
         return [
-            v((128, lanes), BF16),
-            v((128, lanes), BF16),
-            v((128, lanes), F32),
-            v((128, lanes), BF16),
-            v((3, 32, lanes), BF16),
-            v((32, later), BF16),
-            v((8, 16, later), BF16),
-            v((16, later), BF16),
-            v((4, 16, later), BF16),
+            v((32, lanes), BF16),
+            v((8, 16, lanes), BF16),
+            v((16, lanes), BF16),
+            v((4, 16, lanes), BF16),
         ]
 
     return pl.pallas_call(
@@ -685,17 +643,21 @@
             v((256, 384), F32),
             v((256, 128), F32),
             v((128, 128), F32),
+            v((256, 384), BF16),
+            v((7, 32, 384), BF16),
+            v((256, 128), BF16),
+            v((7, 32, 128), BF16),
             v((128, 128), BF16),
             v((7, 16, 128), BF16),
-            *reduction_buffers(384, 384),
-            *reduction_buffers(128, 256),
+            *reduction_buffers(384),
+            *reduction_buffers(256),
             dma((18,)),
             dma((2, 5)),
             dma((2, 5)),
-            dma((14,)),
-            dma((14,)),
             dma((21,)),
             dma((21,)),
+            dma((28,)),
+            dma((28,)),
         ],
         compiler_params=pltpu.CompilerParams(
             collective_id=0, has_side_effects=True, vmem_limit_bytes=STEP_VMEM

time: 39.7 us -> 39.5 us (level)
  no operation moved by 1% of the time
where the time goes in v8:
time: 39.5 us; the launch traced here: 39.4 us
  Pallas kernels  38.7 us (98%)
  between operations  0.64 us (2%)
    pallas_call x1, Pallas kernels, step_call(): pl.pallas_call(step_kernel, out_shape=(jax.ShapeDtypeStruct((2048, 256),...  37.7 us
    pallas_call x1, Pallas kernels, on_device(): pl.pallas_call(unpack_kernel, out_shape=(jax.ShapeDtypeStruct((1, 2, 16,...  1.07 us

profile of v8, /device:TPU:2, one launch (start us, length us, event | category | flops | bytes accessed | tf_op | source)
XLA Modules:
  0.0 39.4 jit_solution(5189201282790423084)
XLA Ops:
  0.6 37.7 %step.1 = (bf16[2048,256]{1,0:T(8,128)(2,1)S(1)}, f32[16,384]{1,0:T(8,128)S(1)}, f32[16,256]{1,0:T(8,128)S(1)}) custom-call(bf16[1,2,8,32,512]{4,3,2,1,0:T(8,128)(2,1)} %x.1, bf16[3,3,3,512,256]{4,3,2,1,0:T(8,128)(2,1)} %w1.1, bf16[3,3,3,256,256]{4,3,2,1,0:T(8,128)(2,1)} %w2.1, bf16[1,2,8,32,256]{4,3,2,1,0:T(8,128)(2,1)} %sl.1, ...), custom_call_target="tpu_custom_call" | custom-call | tf_op jit(solution)/shard_map/step/pallas_call | solution.py:605
  38.3 1.1 %unpack.1 = (bf16[1,2,16,64,256]{4,3,2,1,0:T(8,128)(2,1)}, f32[16,256]{1,0:T(8,128)}, f32[3,3,3,16]{3,2,1,0:T(4,128)}, f32[8,256]{1,0:T(8,128)}, f32[3,3,3,8]{3,2,1,0:T(4,128)}) custom-call(bf16[2048,256]{1,0:T(8,128)(2,1)S(1)} %get-tuple-element.13.mism_s, f32[16,384]{1,0:T(8,128)S(1)} %get-tuple-element.14.low, f32[16,256]{1,0:T(8,128)S(1)} %get-tuple-element.15.high), custom_call_target="tpu_custom_call" | custom-call | tf_op jit(solution)/shard_map/unpack/pallas_call | solution.py:699
